TPU v7x, 256 devices: a whole 4x4x8 slice. The times are simulated.
256 devices in a mesh: dom: 64 (over z_lo, x, y), sub: 4 (over z_hi, core).
Axes of the slice: x: 4, y: 4, z: 8 (z_hi: 2, z_lo: 4; z = z_hi * 4 + z_lo), core: 2. Of those that a mesh axis runs over, the one named last changes fastest.
Arguments:
- positions: bfloat16 [3, 32768], P(None, ('dom', 'sub')), may hold values from 0 to 1
- species: int32 [32768], P(('dom', 'sub')), may hold values from 0 to 1
- neighbours: int32 [64, 32768], P(None, ('dom', 'sub')), may hold values from -1 to 255, as said below
- ghost_rows: int32 [4, 8192], P(None, ('dom', 'sub')), may hold values from 0 to 127
- wavevectors: int32 [3, 12288], replicated, may hold values from -19 to 20, as said below
- embedding: bfloat16 [2, 128], replicated, may hold values from -6 to 6
- w_in: bfloat16 [2, 128, 128], replicated, may hold values from -0.5 to 0.5
- radial: bfloat16 [2, 8, 128], replicated, may hold values from -2 to 2
- norm_gain: bfloat16 [2, 128], replicated, may hold values from 0.25 to 1.75
- w_out: bfloat16 [2, 128, 128], replicated, may hold values from -0.5 to 0.5
- w_charge: bfloat16 [128, 8], replicated, may hold values from -0.5 to 0.5
Outputs:
- potentials: float32 [8, 32768], P(None, ('dom', 'sub'))
- forces: float32 [3, 32768], P(None, ('dom', 'sub'))
Inputs may be any that keep to these rules, and one draw needn't show every extreme that they name: `neighbours`: used slots come first in each atom's list, -1 fills the rest, and every list uses 64 // 2 slots or more; an entry below 128 is one of the device's own atoms, else it is ghost number (entry - 128) % 32 of block (entry - 128) // 32 of the table. `wavevectors`: the columns are distinct; the first nonzero component of each column is positive; the sum of the squares of a column is at most 400.
All inputs are finite; a program needn't handle non-finite values.
Results may differ from a plain program's by a relative error of at most 0.0067.
Values may be sent and summed in bfloat16 or wider, within the bound.
A program may use at most 64 MiB of HBM per device.

v0:
```python
import math

import jax
import jax.numpy as jnp
from jax import lax
from jax.sharding import PartitionSpec as P

smearing = 0.005
epsilon = 1e-05
highest = lax.Precision.HIGHEST


def from_behind(value, axis, steps):
    count = lax.axis_size(axis)
    pairs = [(source, (source + steps) % count) for source in range(count)]
    return lax.ppermute(value, axis, pairs)


def swap_ghosts(outgoing):
    received = []
    for source, offset in ((1, 1), (0, -1)):
        received.append(from_behind(outgoing[source], "dom", offset))
    for source, offset in ((3, 1), (2, -1)):
        received.append(from_behind(outgoing[source], "sub", offset))
    return received


def phase_tile(wave_float, coords, first_k, block_len):
    chosen = lax.dynamic_slice_in_dim(wave_float, first_k, block_len, 1)
    angle = chosen[0][:, None] * coords[0][None, :] + chosen[1][:, None] * coords[1][None, :]
    angle = 2.0 * math.pi * (angle + chosen[2][:, None] * coords[2][None, :])
    return (chosen, jnp.concatenate([jnp.cos(angle), jnp.sin(angle)], axis=0))


def per_device(
    positions,
    species,
    neighbours,
    ghost_rows,
    wavevectors,
    embedding,
    w_in,
    radial,
    norm_gain,
    w_out,
    w_charge,
):
    atom_count = positions.shape[1]
    channels = w_in.shape[2]
    coords = positions.astype(jnp.float32)
    ghost_coords = swap_ghosts([positions[:, ghost_rows[side_number]] for side_number in range(4)])
    coord_table = jnp.concatenate([positions] + ghost_coords, axis=1).astype(jnp.float32)
    clamped = jnp.maximum(neighbours, 0)
    live_mask = (neighbours >= 0)[:, :, None]
    nearby = coord_table[:, clamped]
    displace = nearby - coords[:, None, :]
    chord_sq = jnp.sum(jnp.sin(math.pi * displace) ** 2, axis=0)
    decay_rates = jnp.exp2(jnp.arange(radial.shape[1], dtype=jnp.float32) - 3.0)
    radial_basis = jnp.exp(-decay_rates[:, None, None] * chord_sq[None, :, :])
    atom_block = math.gcd(atom_count, 256)
    hidden = jnp.where((species == 1)[:, None], embedding[1][None, :], embedding[0][None, :])
    for layer_number in range(w_in.shape[0]):
        projected = jnp.dot(hidden, w_in[layer_number], preferred_element_type=jnp.float32).astype(
            jnp.bfloat16
        )
        ghost_feats = swap_ghosts([projected[ghost_rows[side_number]] for side_number in range(4)])
        feat_table = jnp.concatenate([projected] + ghost_feats, axis=0)
        radial_layer = radial[layer_number].astype(jnp.float32)

        def message_block(block_number, message, feat_table=feat_table, radial_layer=radial_layer):
            edge_weight = jnp.einsum("bna,bc->nac", radial_basis, radial_layer, precision=highest)
            gathered = feat_table[clamped].astype(jnp.float32)
            part_sum = jnp.sum(jnp.where(live_mask, edge_weight * gathered, 0.0), axis=0)
            return part_sum

        message = lax.fori_loop(
            0,
            atom_count // atom_block,
            message_block,
            jnp.zeros((atom_count, channels), jnp.float32),
        )
        normed = message * lax.rsqrt(jnp.mean(message * message, axis=1, keepdims=True) + epsilon)
        normed = normed * norm_gain[layer_number].astype(jnp.float32)[None, :]
        activated = jax.nn.silu(normed).astype(jnp.bfloat16)
        update = jnp.dot(activated, w_out[layer_number], preferred_element_type=jnp.float32)
        hidden = (hidden.astype(jnp.float32) + update).astype(jnp.bfloat16)
    charges = jnp.dot(
        hidden.astype(jnp.float32),
        w_charge.astype(jnp.float32),
        precision=highest,
        preferred_element_type=jnp.float32,
    ).T
    latent = charges.shape[0]
    wave_float = wavevectors.astype(jnp.float32)
    total_k = wave_float.shape[1]
    block_len = math.gcd(total_k, 512)
    block_count = total_k // block_len
    squared = jnp.sum(wave_float * wave_float, axis=0)
    kweight = jnp.exp(-smearing * squared) / squared

    def accumulate(block_number, structure):
        first_k = block_number * block_len
        chosen, tile = phase_tile(wave_float, coords, first_k, block_len)
        piece = lax.dot_general(
            charges,
            tile,
            (((1,), (1,)), ((), ())),
            precision=highest,
            preferred_element_type=jnp.float32,
        )
        piece = jnp.concatenate([piece[:, :block_len], piece[:, block_len:]], axis=0)
        return lax.dynamic_update_slice_in_dim(structure, piece, first_k, 1)

    structure = lax.fori_loop(
        0, block_count, accumulate, jnp.zeros((2 * latent, total_k), jnp.float32)
    )
    weighted = lax.psum(structure, ("dom", "sub")) * kweight[None, :]

    def apply_block(block_number, carry):
        potential, force_sum = carry
        first_k = block_number * block_len
        chosen, tile = phase_tile(wave_float, coords, first_k, block_len)
        cos_weight = lax.dynamic_slice(weighted, (0, first_k), (latent, block_len))
        sin_weight = lax.dynamic_slice(weighted, (latent, first_k), (latent, block_len))
        force_left = jnp.concatenate(
            [
                -(chosen[:, None, :] * sin_weight[None, :, :]),
                chosen[:, None, :] * cos_weight[None, :, :],
            ],
            axis=2,
        )
        left_rows = jnp.concatenate(
            [
                jnp.concatenate([cos_weight, sin_weight], axis=1),
                force_left.reshape(3 * latent, 2 * block_len),
            ],
            axis=0,
        )
        product = jnp.dot(left_rows, tile, precision=highest, preferred_element_type=jnp.float32)
        potential = potential + product[:latent]
        inner_terms = product[latent:].reshape(3, latent, atom_count)
        force_sum = force_sum + jnp.sum(charges[None, :, :] * inner_terms, axis=1)
        return (potential, force_sum)

    start = (jnp.zeros((latent, atom_count), jnp.float32), jnp.zeros((3, atom_count), jnp.float32))
    potential, force_sum = lax.fori_loop(0, block_count, apply_block, start)
    scale = 1.0 / math.sqrt(atom_count * lax.axis_size(("dom", "sub")))
    return (potential * scale, force_sum * scale)


def solution(mesh):
    return jax.shard_map(
        per_device,
        mesh=mesh,
        in_specs=(
            P(None, ("dom", "sub")),
            P(("dom", "sub")),
            P(None, ("dom", "sub")),
            P(None, ("dom", "sub")),
            P(),
            P(),
            P(),
            P(),
            P(),
            P(),
            P(),
        ),
        out_specs=(P(None, ("dom", "sub")), P(None, ("dom", "sub"))),
        check_vma=False,
    )
```

profile of v0, /device:TPU:1, one launch (start us, length us, event | category | flops | bytes accessed | tf_op | source)
XLA Modules:
  0.0 504.8 jit_solution(10311800674291252774)
XLA Ops:
  11.0 2.2 collective-permute-start.4
  13.8 7.8 %collective-permute-start.5 = (bf16[32,128]{1,0:T(8,128)(2,1)S(1)}, bf16[32,128]{1,0:T(8,128)(2,1)S(1)}, u32[]{:S(2)}, u32[]{:S(2)}) collective-permute-start(bf16[32,128]{1,0:T(8,128)(2,1)S(1)} %gather_fusion.6), channel_id=1, source_target_pairs={{0,252},{4,0},{8,4},{12,8},{16,12},{20,16},{24,20},{28,24},{32,28}... | collective-permute-start | bytes 24584 | tf_op jit(solution)/shard_map/ppermute | solution.py:16
  22.2 6.6 %collective-permute-start.6 = (bf16[32,128]{1,0:T(8,128)(2,1)S(1)}, bf16[32,128]{1,0:T(8,128)(2,1)S(1)}, u32[]{:S(2)}, u32[]{:S(2)}) collective-permute-start(bf16[32,128]{1,0:T(8,128)(2,1)S(1)} %gather_fusion.7), channel_id=1, source_target_pairs={{0,1},{1,2},{2,3},{3,0},{4,5},{5,6},{6,7},{7,4},{8,9},{9,10},{10,1... | collective-permute-start | bytes 24584 | tf_op jit(solution)/shard_map/ppermute | solution.py:16
  30.9 7.5 %collective-permute-start.1 = (bf16[3,32]{0,1:T(8,128)(2,1)S(1)}, bf16[3,32]{0,1:T(8,128)(2,1)S(1)}, u32[]{:S(2)}, u32[]{:S(2)}) collective-permute-start(bf16[3,32]{0,1:T(8,128)(2,1)S(1)} %bitcast.142), channel_id=1, source_target_pairs={{0,252},{4,0},{8,4},{12,8},{16,12},{20,16},{24,20},{28,24},{32,28}... | collective-permute-start | bytes 584 | tf_op jit(solution)/shard_map/ppermute | solution.py:16
  43.4 1.1 multiply_reduce_fusion
  45.9 1.1 collective-permute-start.7
  47.2 5.1 %collective-permute-done.3 = bf16[3,32]{0,1:T(8,128)(2,1)S(1)} collective-permute-done((bf16[3,32]{0,1:T(8,128)(2,1)S(1)}, bf16[3,32]{0,1:T(8,128)(2,1)S(1)}, u32[]{:S(2)}, u32[]{:S(2)}) %collective-permute-start.3) | collective-permute-done | bytes 224 | tf_op jit(solution)/shard_map/ppermute | solution.py:16
  53.2 27.7 %gather_fusion.4 = f32[8192,3]{1,0:T(8,128)} fusion(f32[3,256]{0,1:T(8,128)S(1)} %copy.47, s32[8192]{0:T(1024)S(1)} %bitcast_clamp_fusion), kind=kCustom, calls=%fused_computation.4 | custom fusion | bytes 229376 | tf_op jit(solution)/shard_map/gather | solution.py:55
  80.9 2.8 copy.49
  84.1 5.1 %fusion.29 = f32[64,128,128]{2,1,0:T(8,128)} fusion(f32[64,128]{1,0:T(8,128)S(1)} %fusion.37, f32[8]{0:T(128)S(1)} %exponential_negate_fusion, bf16[2,8,128]{2,1,0:T(8,128)(2,1)S(1)} %copy-done.3), kind=kOutput, calls=%fused_computation.73 | convolution fusion | flops 100728832 | bytes 4229632 | tf_op jit(solution)/shard_map/while/body/eval_jaxpr/bna,bc->nac/dot_general | solution.py:71
  89.3 24.0 %gather_fusion.9 = bf16[8192,128]{1,0:T(8,128)(2,1)S(1)} fusion(bf16[256,128]{1,0:T(8,128)(2,1)S(1)} %constant_dynamic-update-slice_fusion, s32[8192]{0:T(1024)S(1)} %bitcast_clamp_fusion), kind=kCustom, calls=%fused_computation.9 | custom fusion | bytes 4227072 | tf_op jit(solution)/shard_map/while/body/eval_jaxpr/gather | solution.py:72
  113.4 3.7 fusion.25
  118.4 5.1 %fusion.28 = f32[64,128,128]{2,1,0:T(8,128)} fusion(f32[64,128]{1,0:T(8,128)S(1)} %fusion.37, f32[8]{0:T(128)S(1)} %exponential_negate_fusion, bf16[2,8,128]{2,1,0:T(8,128)(2,1)S(1)} %copy-done.3), kind=kOutput, calls=%fused_computation.72 | convolution fusion | flops 100728832 | bytes 4229632 | tf_op jit(solution)/shard_map/while/body/eval_jaxpr/bna,bc->nac/dot_general | solution.py:71
  125.3 7.5 %collective-permute-start.9 = (bf16[32,128]{1,0:T(8,128)(2,1)S(1)}, bf16[32,128]{1,0:T(8,128)(2,1)S(1)}, u32[]{:S(2)}, u32[]{:S(2)}) collective-permute-start(bf16[32,128]{1,0:T(8,128)(2,1)S(1)} %gather_fusion.11), channel_id=1, source_target_pairs={{0,252},{4,0},{8,4},{12,8},{16,12},{20,16},{24,20},{28,24},{32,28}... | collective-permute-start | bytes 24584 | tf_op jit(solution)/shard_map/ppermute | solution.py:16
  134.3 6.2 %collective-permute-done.11 = bf16[32,128]{1,0:T(8,128)(2,1)S(1)} collective-permute-done((bf16[32,128]{1,0:T(8,128)(2,1)S(1)}, bf16[32,128]{1,0:T(8,128)(2,1)S(1)}, u32[]{:S(2)}, u32[]{:S(2)}) %collective-permute-start.11) | collective-permute-done | bytes 8224 | tf_op jit(solution)/shard_map/ppermute | solution.py:16
  140.5 24.0 %gather_fusion.14 = bf16[8192,128]{1,0:T(8,128)(2,1)S(1)} fusion(bf16[256,128]{1,0:T(8,128)(2,1)S(1)} %constant_dynamic-update-slice_fusion.5, s32[8192]{0:T(1024)S(1)} %bitcast_clamp_fusion), kind=kCustom, calls=%fused_computation.14 | custom fusion | bytes 4227072 | tf_op jit(solution)/shard_map/while/body/eval_jaxpr/gather | solution.py:72
  164.5 3.6 fusion.23
  168.7 41.6 %while.18 = (s32[]{:T(128)}, f32[16,12288]{1,0:T(8,128)S(1)}, f32[3,12288]{1,0:T(4,128)S(1)}, f32[3,128]{1,0:T(4,128)S(1)}, f32[8,128]{1,0:T(8,128)S(1)}, /*inde...) while((s32[]{:T(128)}, f32[16,12288]{1,0:T(8,128)S(1)}, f32[3,12288]{1,0:T(4,128)S(1)}, ...), condition=%wide.region_6.7_spmd, body=%wide.region_5.6_spmd.sunk | while | flops 13115400 | bytes 1239747 | solution.py:114
  168.8 1.0 fusion.82
  170.6 1.0 fusion.82
  172.3 1.0 fusion.82
  174.0 1.0 fusion.82
  175.8 1.0 fusion.82
  177.5 1.0 fusion.82
  182.7 1.0 fusion.82
  207.0 1.0 fusion.82
  211.3 244.3 %all-reduce.2.cloned.1.call-done = f32[16,12288]{1,0:T(8,128)} async-done(((f32[16,12288]{1,0:T(8,128)}), f32[16,12288]{1,0:T(8,128)}) %all-reduce.2.cloned.1.call-update) | async-done | bytes 786448 | tf_op jit(solution)/shard_map/psum | solution.py:117
  455.6 1.2 broadcast_multiply_fusion
  456.8 40.0 %while.38 = (s32[]{:T(128)}, f32[8,128]{1,0:T(8,128)S(1)}, f32[3,128]{1,0:T(4,128)S(1)}, f32[16,12288]{1,0:T(8,128)S(1)}, f32[3,12288]{1,0:T(4,128)S(1)}, /*inde...) while((s32[]{:T(128)}, f32[8,128]{1,0:T(8,128)S(1)}, ...), condition=%wide.region_11.12_spmd.clone, body=%wide.region_9.11_spmd.clone.sunk | while | flops 50999688 | bytes 1469154 | solution.py:146
  460.2 1.0 fusion.86
  468.6 1.0 fusion.86
  491.9 1.0 fusion.86
  (456 shorter events, 89.6 us)
Async XLA Ops:
  7.2 161.3 %copy-start = (bf16[128,8]{0,1:T(8,128)(2,1)S(1)}, bf16[128,8]{0,1:T(8,128)(2,1)}, u32[]{:S(2)}) copy-start(bf16[128,8]{0,1:T(8,128)(2,1)} %param.25) | copy-start | bytes 6148
  7.2 77.0 %copy-start.3 = (bf16[2,8,128]{2,1,0:T(8,128)(2,1)S(1)}, bf16[2,8,128]{2,1,0:T(8,128)(2,1)}, u32[]{:S(2)}) copy-start(bf16[2,8,128]{2,1,0:T(8,128)(2,1)} %param.22) | copy-start | bytes 12292
  7.2 448.4 %all-reduce.2.cloned.1.call-start = ((), (), s32[]{:S(2)}) async-start(), calls=%async_computation | async-start | bytes 1572864 | tf_op jit(solution)/shard_map/psum | solution.py:117
  11.0 78.2 %collective-permute-start.4 = (bf16[32,128]{1,0:T(8,128)(2,1)S(1)}, bf16[32,128]{1,0:T(8,128)(2,1)S(1)}, u32[]{:S(2)}, u32[]{:S(2)}) collective-permute-start(bf16[32,128]{1,0:T(8,128)(2,1)S(1)} %gather_fusion.5), channel_id=1, source_target_pairs={{0,4},{4,8},{8,12},{12,16},{16,20},{20,24},{24,28},{28,32},{32,36}... | collective-permute-start | bytes 24584 | tf_op jit(solution)/shard_map/ppermute | solution.py:16
  13.8 75.4 %collective-permute-start.5 = (bf16[32,128]{1,0:T(8,128)(2,1)S(1)}, bf16[32,128]{1,0:T(8,128)(2,1)S(1)}, u32[]{:S(2)}, u32[]{:S(2)}) collective-permute-start(bf16[32,128]{1,0:T(8,128)(2,1)S(1)} %gather_fusion.6), channel_id=1, source_target_pairs={{0,252},{4,0},{8,4},{12,8},{16,12},{20,16},{24,20},{28,24},{32,28}... | collective-permute-start | bytes 24584 | tf_op jit(solution)/shard_map/ppermute | solution.py:16
  22.2 67.1 %collective-permute-start.6 = (bf16[32,128]{1,0:T(8,128)(2,1)S(1)}, bf16[32,128]{1,0:T(8,128)(2,1)S(1)}, u32[]{:S(2)}, u32[]{:S(2)}) collective-permute-start(bf16[32,128]{1,0:T(8,128)(2,1)S(1)} %gather_fusion.7), channel_id=1, source_target_pairs={{0,1},{1,2},{2,3},{3,0},{4,5},{5,6},{6,7},{7,4},{8,9},{9,10},{10,1... | collective-permute-start | bytes 24584 | tf_op jit(solution)/shard_map/ppermute | solution.py:16
  30.2 14.3 %collective-permute-start = (bf16[3,32]{0,1:T(8,128)(2,1)S(1)}, bf16[3,32]{0,1:T(8,128)(2,1)S(1)}, u32[]{:S(2)}, u32[]{:S(2)}) collective-permute-start(bf16[3,32]{0,1:T(8,128)(2,1)S(1)} %bitcast.143), channel_id=1, source_target_pairs={{0,4},{4,8},{8,12},{12,16},{16,20},{20,24},{24,28},{28,32},{32,36}... | collective-permute-start | bytes 584 | tf_op jit(solution)/shard_map/ppermute | solution.py:16
  30.9 14.4 %collective-permute-start.1 = (bf16[3,32]{0,1:T(8,128)(2,1)S(1)}, bf16[3,32]{0,1:T(8,128)(2,1)S(1)}, u32[]{:S(2)}, u32[]{:S(2)}) collective-permute-start(bf16[3,32]{0,1:T(8,128)(2,1)S(1)} %bitcast.142), channel_id=1, source_target_pairs={{0,252},{4,0},{8,4},{12,8},{16,12},{20,16},{24,20},{28,24},{32,28}... | collective-permute-start | bytes 584 | tf_op jit(solution)/shard_map/ppermute | solution.py:16
  44.5 1.4 collective-permute-start.2
  45.2 7.0 %collective-permute-start.3 = (bf16[3,32]{0,1:T(8,128)(2,1)S(1)}, bf16[3,32]{0,1:T(8,128)(2,1)S(1)}, u32[]{:S(2)}, u32[]{:S(2)}) collective-permute-start(bf16[3,32]{0,1:T(8,128)(2,1)S(1)} %bitcast.140), channel_id=1, source_target_pairs={{0,3},{1,0},{2,1},{3,2},{4,7},{5,4},{6,5},{7,6},{8,11},{9,8},{10,9... | collective-permute-start | bytes 584 | tf_op jit(solution)/shard_map/ppermute | solution.py:16
  45.9 43.4 %collective-permute-start.7 = (bf16[32,128]{1,0:T(8,128)(2,1)S(1)}, bf16[32,128]{1,0:T(8,128)(2,1)S(1)}, u32[]{:S(2)}, u32[]{:S(2)}) collective-permute-start(bf16[32,128]{1,0:T(8,128)(2,1)S(1)} %gather_fusion.8), channel_id=1, source_target_pairs={{0,3},{1,0},{2,1},{3,2},{4,7},{5,4},{6,5},{7,6},{8,11},{9,8},{10,9... | collective-permute-start | bytes 24584 | tf_op jit(solution)/shard_map/ppermute | solution.py:16
  113.4 3.8 copy-start.4
  113.4 4.0 copy-start.2
  118.2 15.3 %collective-permute-start.8 = (bf16[32,128]{1,0:T(8,128)(2,1)S(1)}, bf16[32,128]{1,0:T(8,128)(2,1)S(1)}, u32[]{:S(2)}, u32[]{:S(2)}) collective-permute-start(bf16[32,128]{1,0:T(8,128)(2,1)S(1)} %gather_fusion.10), channel_id=1, source_target_pairs={{0,4},{4,8},{8,12},{12,16},{16,20},{20,24},{24,28},{28,32},{32,36}... | collective-permute-start | bytes 24584 | tf_op jit(solution)/shard_map/ppermute | solution.py:16
  125.3 8.3 %collective-permute-start.9 = (bf16[32,128]{1,0:T(8,128)(2,1)S(1)}, bf16[32,128]{1,0:T(8,128)(2,1)S(1)}, u32[]{:S(2)}, u32[]{:S(2)}) collective-permute-start(bf16[32,128]{1,0:T(8,128)(2,1)S(1)} %gather_fusion.11), channel_id=1, source_target_pairs={{0,252},{4,0},{8,4},{12,8},{16,12},{20,16},{24,20},{28,24},{32,28}... | collective-permute-start | bytes 24584 | tf_op jit(solution)/shard_map/ppermute | solution.py:16
  132.9 1.4 collective-permute-start.10
  133.5 7.0 %collective-permute-start.11 = (bf16[32,128]{1,0:T(8,128)(2,1)S(1)}, bf16[32,128]{1,0:T(8,128)(2,1)S(1)}, u32[]{:S(2)}, u32[]{:S(2)}) collective-permute-start(bf16[32,128]{1,0:T(8,128)(2,1)S(1)} %gather_fusion.13), channel_id=1, source_target_pairs={{0,3},{1,0},{2,1},{3,2},{4,7},{5,4},{6,5},{7,6},{8,11},{9,8},{10,9... | collective-permute-start | bytes 24584 | tf_op jit(solution)/shard_map/ppermute | solution.py:16
  210.3 0.9 copy-start.1
Sparse Core Ops, SparseCore 0:
  211.4 244.1 all-reduce.1
where the time goes:
time: 506 us; the launch traced here: 505 us
  waiting for transfers between devices  257 us (51%)
  local copies, waits for them, and re-layouts  93.8 us (19%)
  other arithmetic  68.2 us (13%)
  starting transfers between devices  34.4 us (7%)
  matrix products  34.4 us (7%)
  between operations  14.3 us (3%)
    psum x1, waiting for transfers between devices, per_device(): weighted = lax.psum(structure, ('dom', 'sub')) * kweight[None, :]  244 us
    cos x48, other arithmetic, phase_tile(): return (chosen, jnp.concatenate([jnp.cos(angle), jnp.sin(angle)], axis=0))  49.8 us
    gather x2, local copies, waits for them, and re-layouts, message_block(): gathered = feat_table[clamped].astype(jnp.float32)  48 us
    ppermute x12, starting transfers between devices, from_behind(): return lax.ppermute(value, axis, pairs)  34.4 us
    gather x2, local copies, waits for them, and re-layouts, per_device(): nearby = coord_table[:, clamped]  30.5 us
    dot_general x24, matrix products, accumulate(): lax.dot_general(charges, tile, (((1,), (1,)), ((), ())), precision=highes...  13.1 us
    ppermute x12, waiting for transfers between devices, from_behind(): return lax.ppermute(value, axis, pairs)  12.6 us
    dot_general x2, matrix products, message_block(): jnp.einsum('bna,bc->nac', radial_basis, radial_layer, precision=highest)  10.2 us
  transfers between devices with their start and end apart: 13, of which 6 were waited for; matrix products, arithmetic and copies ran while one was open for 11% of the time, Pallas kernels for 0%

commit v1 on v0

v1 whole, which is shorter than its diff:
```python
import functools
import math

import jax
import jax.numpy as jnp
import numpy as np
from jax import lax
from jax.experimental import pallas as pl
from jax.experimental.pallas import tpu as pltpu
from jax.sharding import PartitionSpec as P

MESH = pl.DeviceIdType.MESH
smearing = 0.005
epsilon = 1e-05
f32 = jnp.float32
bf16 = jnp.bfloat16
plane = 16
members = 2 * plane
depth = 8
round_magic = 12582912.0


def fit_series(function, terms):
    nodes = (np.cos(np.pi * (np.arange(4 * terms) + 0.5) / (4 * terms)) + 1.0) / 8.0
    fitted = np.polynomial.chebyshev.Chebyshev.fit(nodes, function(np.sqrt(nodes)), terms - 1, domain=[0.0, 0.25])
    return [float(c) for c in fitted.convert(kind=np.polynomial.Polynomial).coef]


def cos_series(terms):
    return fit_series(lambda t: np.cos(2.0 * np.pi * t), terms)


def sin_series(terms):
    return fit_series(lambda t: np.sin(2.0 * np.pi * t) / t, terms)


def horner(coefs, u):
    value = coefs[-1]
    for c in coefs[-2::-1]:
        value = value * u + c
    return value


def turns_cos_sin(turns, cos_coefs, sin_coefs):
    t = turns - ((turns + round_magic) - round_magic)
    u = t * t
    return horner(cos_coefs, u), t * horner(sin_coefs, u)


def dot_nt(a, b):
    return lax.dot_general(a, b, (((1,), (1,)), ((), ())), preferred_element_type=f32)


def dot_nn(a, b):
    return jnp.dot(a, b, preferred_element_type=f32)


def kernel(
    scale,
    pos_ref, spec_ref, nbr_ref, gr_ref, wv_ref, emb_ref, win_ref, rad_ref, gain_ref, wout_ref, wch_ref,
    pot_ref, force_ref,
    c32, coords, ghost_out, ghost_in, gpad, pos_all, q_all, wv32, wvb, wvt,
    cos_s, sin_s, cos_a, sin_a, m_ref, feat_out, feat_in, z_out, z_in, z_full,
    g1_send, g1_recv, g2_send, g2_recv, p_send, p_recv, q_send, q_recv,
    zs_send, zs_recv, w_send, w_recv, x_send, x_recv,
):
    dom = lax.axis_index("dom")
    sub = lax.axis_index("sub")
    n_dom = lax.axis_size("dom")
    n_sub = lax.axis_size("sub")
    zl, xy = dom // plane, lax.rem(dom, plane)
    zh, core = sub // 2, lax.rem(sub, 2)
    me = core * plane + xy
    z_me = zh * (depth // 2) + zl
    atoms = pos_ref.shape[1]
    total_k = wv_ref.shape[1]
    share = total_k // members
    latent = wch_ref.shape[1]
    bases = rad_ref.shape[1]
    ghosts = gr_ref.shape[1]

    def member(index):
        return (zl * plane + lax.rem(index, plane), zh * 2 + index // plane)

    def column_member(index):
        return (lax.rem(index, depth // 2) * plane + xy, (index // (depth // 2)) * 2 + core)

    neighbours_at = (
        (lax.rem(dom + 1, n_dom), sub),
        (lax.rem(dom + n_dom - 1, n_dom), sub),
        (dom, lax.rem(sub + 1, n_sub)),
        (dom, lax.rem(sub + n_sub - 1, n_sub)),
    )

    barrier = pltpu.get_barrier_semaphore()
    for target in neighbours_at:
        pl.semaphore_signal(barrier, inc=1, device_id=target, device_id_type=MESH)

    @pl.loop(1, members)
    def _(o):
        pl.semaphore_signal(barrier, inc=1, device_id=member(lax.rem(me + o, members)), device_id_type=MESH)

    @pl.loop(1, depth)
    def _(o):
        pl.semaphore_signal(barrier, inc=1, device_id=column_member(lax.rem(z_me + o, depth)), device_id_type=MESH)

    c32[...] = jnp.zeros_like(c32)
    c32[0:3, :] = pos_ref[...].astype(f32)
    c32[3:4, :] = spec_ref[...].astype(f32)
    coords[...] = c32[...].astype(bf16)
    gpad[...] = jnp.zeros_like(gpad)
    gpad[0:4, 0:ghosts] = gr_ref[...].astype(f32)
    grown = gpad[...]
    picks = grown[1:2, :]
    for block, source in ((1, 0), (2, 3), (3, 2)):
        picks = picks + pltpu.roll(grown, block * ghosts, axis=1)[source:source + 1, :]
    row_number = lax.broadcasted_iota(jnp.int32, (atoms, atoms), 0).astype(f32)
    pick_cols = jnp.where(row_number == picks, 1.0, 0.0)
    ghost_out[...] = dot_nn(coords[...], pick_cols.astype(bf16)).astype(bf16)
    my_lanes = pl.ds(pl.multiple_of(me * atoms, atoms), atoms)
    pos_all[:, my_lanes] = coords[...]

    def ghost_copy(block):
        return pltpu.make_async_remote_copy(
            src_ref=ghost_out, dst_ref=ghost_in.at[block], send_sem=g1_send.at[block], recv_sem=g1_recv.at[block],
            device_id=neighbours_at[block], device_id_type=MESH)

    def feat_copy(block):
        rows = pl.ds(block * ghosts, ghosts)
        return pltpu.make_async_remote_copy(
            src_ref=feat_out.at[rows], dst_ref=feat_in.at[rows], send_sem=g2_send.at[block], recv_sem=g2_recv.at[block],
            device_id=neighbours_at[block], device_id_type=MESH)

    def spread_copy(o, buffer, send, recv, slot):
        lanes = pl.ds(pl.multiple_of(slot * atoms, atoms), atoms)
        return pltpu.make_async_remote_copy(
            src_ref=buffer.at[:, lanes], dst_ref=buffer.at[:, lanes], send_sem=send.at[o], recv_sem=recv.at[o],
            device_id=member(lax.rem(me + o, members)), device_id_type=MESH)

    def spread_start(buffer, send, recv):
        @pl.loop(1, members)
        def _(o):
            spread_copy(o, buffer, send, recv, me).start()

    def spread_wait(buffer, send, recv):
        @pl.loop(1, members)
        def _(o):
            spread_copy(o, buffer, send, recv, lax.rem(me + members - o, members)).wait_recv()

    def spread_sent(buffer, send, recv):
        @pl.loop(1, members)
        def _(o):
            spread_copy(o, buffer, send, recv, me).wait_send()

    def column_copy(o):
        return pltpu.make_async_remote_copy(
            src_ref=z_out, dst_ref=z_in.at[o], send_sem=zs_send.at[o], recv_sem=zs_recv.at[o],
            device_id=column_member(lax.rem(z_me + o, depth)), device_id_type=MESH)

    def share_lanes(which_core, which_xy):
        first = (which_core * plane + which_xy) * share
        return pl.ds(pl.multiple_of(first, 128), share)

    def plane_copy(o, from_xy):
        lanes = share_lanes(core, from_xy)
        return pltpu.make_async_remote_copy(
            src_ref=z_full.at[:, lanes], dst_ref=z_full.at[:, lanes], send_sem=w_send.at[o], recv_sem=w_recv.at[o],
            device_id=(zl * plane + lax.rem(xy + o, plane), sub), device_id_type=MESH)

    def twin_copy(o, from_core):
        lanes = share_lanes(from_core, lax.rem(xy + plane - o, plane))
        return pltpu.make_async_remote_copy(
            src_ref=z_full.at[:, lanes], dst_ref=z_full.at[:, lanes], send_sem=x_send.at[o], recv_sem=x_recv.at[o],
            device_id=(dom, zh * 2 + 1 - core), device_id_type=MESH)

    pl.semaphore_wait(barrier, 4 + (members - 1) + (depth - 1))
    for block in range(4):
        ghost_copy(block).start()
    spread_start(pos_all, p_send, p_recv)

    table_row = lax.broadcasted_iota(jnp.int32, (2 * atoms, atoms), 0)

    def tally(step, counted):
        for inner in range(8):
            counted = counted + jnp.where(table_row == nbr_ref[pl.ds(step * 8 + inner, 1), :], 1.0, 0.0)
        return counted

    counted = lax.fori_loop(0, nbr_ref.shape[0] // 8, tally, jnp.zeros((2 * atoms, atoms), f32))
    counts = (counted[:atoms].T, counted[atoms:].T)
    pick_rows = pick_cols.T.astype(bf16)

    wv32[...] = jnp.zeros_like(wv32)
    wv32[0:3, :] = wv_ref[...].astype(f32)
    wvb[...] = wv32[...].astype(bf16)
    own_share = pl.ds(pl.multiple_of(me * share, 128), share)
    own_waves = wv32[:, own_share]
    wvt[...] = own_waves.T.astype(bf16)
    squared = jnp.sum(own_waves * own_waves, axis=0, keepdims=True)
    kweight = jnp.exp(-smearing * squared) / squared * scale

    cos_fine, sin_fine = cos_series(9), sin_series(9)
    cos_fast, sin_fast = cos_series(6), sin_series(5)

    own32 = c32[...]
    own_cos, own_sin = turns_cos_sin(0.5 * own32, cos_fine, sin_fine)
    own_cos_col, own_sin_col = own_cos.T, own_sin.T
    own_col = own32.T
    pos_col = own_col.astype(bf16)
    embedding = emb_ref[...].astype(f32)
    gains = gain_ref[...].astype(f32)
    is_second = own_col[:, 3:4] > 0.5
    hidden = jnp.where(is_second, embedding[1:2, :], embedding[0:1, :])
    both = lax.broadcasted_iota(jnp.int32, (16, embedding.shape[1]), 0)
    both = jnp.where(both == 1, embedding[1:2, :], embedding[0:1, :]).astype(bf16)
    projected_kinds = dot_nn(both, win_ref[0]).astype(bf16).astype(f32)
    own_feats = jnp.where(is_second, projected_kinds[1:2, :], projected_kinds[0:1, :])
    charge_rows = wch_ref[...].astype(f32).T.astype(bf16)

    def fill_pairs(half, table_cos, table_sin):
        chord = jnp.zeros((atoms, atoms), f32)
        for d in range(3):
            apart = table_sin[d:d + 1, :] * own_cos_col[:, d:d + 1] - table_cos[d:d + 1, :] * own_sin_col[:, d:d + 1]
            chord = chord + apart * apart
        for b in range(bases):
            pair = counts[half] * jnp.exp(-(2.0 ** (b - 3)) * chord)
            high = pair.astype(bf16)
            rows = slice(b * atoms, (b + 1) * atoms)
            m_ref[rows, half * atoms:(half + 1) * atoms] = high
            m_ref[rows, (half + 2) * atoms:(half + 3) * atoms] = (pair - high.astype(f32)).astype(bf16)

    def layer(number, hidden, table):
        products = dot_nn(m_ref[...], jnp.concatenate([table, table], axis=0))
        radial_layer = rad_ref[number].astype(f32)
        message = radial_layer[0:1, :] * products[:atoms]
        for b in range(1, bases):
            message = message + radial_layer[b:b + 1, :] * products[b * atoms:(b + 1) * atoms]
        normed = message * lax.rsqrt(jnp.mean(message * message, axis=1, keepdims=True) + epsilon)
        normed = normed * gains[number:number + 1, :]
        activated = (normed / (1.0 + jnp.exp(-normed))).astype(bf16)
        update = dot_nn(activated, wout_ref[number])
        return (hidden + update).astype(bf16).astype(f32)

    fill_pairs(0, own_cos, own_sin)

    for block in range(4):
        ghost_copy(block).wait_recv()
    lane_block = lax.broadcasted_iota(jnp.int32, (16, atoms), 1) // ghosts
    ghost32 = jnp.zeros((16, atoms), f32)
    for block in range(4):
        ghost32 = jnp.where(lane_block == block, ghost_in[block].astype(f32), ghost32)
    ghost_cos, ghost_sin = turns_cos_sin(0.5 * ghost32, cos_fine, sin_fine)
    fill_pairs(1, ghost_cos, ghost_sin)
    ghost_second = ghost32.T[:, 3:4] > 0.5
    ghost_feats = jnp.where(ghost_second, projected_kinds[1:2, :], projected_kinds[0:1, :])
    table = jnp.concatenate([own_feats, ghost_feats], axis=0).astype(bf16)
    hidden = layer(0, hidden, table)
    projected = dot_nn(hidden.astype(bf16), win_ref[1]).astype(bf16)
    feat_out[...] = dot_nn(pick_rows, projected).astype(bf16)
    for block in range(4):
        feat_copy(block).start()

    spread_wait(pos_all, p_send, p_recv)

    def share_phases(step):
        lanes = pl.ds(pl.multiple_of(step * 256, 256), 256)
        for first in range(0, share, 64):
            rows = slice(first, first + 64)
            cosines, sines = turns_cos_sin(dot_nn(wvt[rows, :], pos_all[:, lanes]), cos_fast, sin_fast)
            cos_s[rows, lanes] = cosines.astype(bf16)
            sin_s[rows, lanes] = sines.astype(bf16)

    def atom_phases(step):
        lanes = pl.ds(pl.multiple_of(step * 256, 256), 256)
        for first in range(0, atoms, 64):
            rows = slice(first, first + 64)
            cosines, sines = turns_cos_sin(dot_nn(pos_col[rows, :], wvb[:, lanes]), cos_fast, sin_fast)
            cos_a[rows, lanes] = cosines.astype(bf16)
            sin_a[rows, lanes] = sines.astype(bf16)

    share_steps = members * atoms // 256
    atom_steps = total_k // 256
    pl.loop(0, share_steps // 2)(share_phases)

    for block in range(4):
        feat_copy(block).wait_recv()
    table = jnp.concatenate([projected, feat_in[...]], axis=0)
    hidden = layer(1, hidden, table)
    charges = dot_nt(charge_rows, hidden.astype(bf16))
    charges_high = charges.astype(bf16).astype(f32)
    q_all[:, my_lanes] = jnp.concatenate([charges_high, charges - charges_high], axis=0).astype(bf16)
    spread_start(q_all, q_send, q_recv)
    pl.loop(share_steps // 2, share_steps)(share_phases)
    spread_wait(q_all, q_send, q_recv)

    by_cos = dot_nt(q_all[...], cos_s[...])
    by_sin = dot_nt(q_all[...], sin_s[...])
    partial = jnp.concatenate([by_cos[:latent] + by_cos[latent:], by_sin[:latent] + by_sin[latent:]], axis=0) * kweight
    z_out[...] = partial.astype(bf16)

    @pl.loop(1, depth)
    def _(o):
        column_copy(o).start()

    pl.loop(0, atom_steps // 2)(atom_phases)

    @pl.loop(1, depth)
    def _(o):
        column_copy(o).wait_recv()

    summed = z_out[...].astype(f32)
    for o in range(1, depth):
        summed = summed + z_in[o].astype(f32)
    z_full[:, share_lanes(core, xy)] = summed.astype(bf16)

    @pl.loop(1, plane)
    def _(o):
        plane_copy(o, xy).start()

    twin_copy(0, core).start()
    pl.loop(atom_steps // 2, atom_steps)(atom_phases)

    @pl.loop(1, plane)
    def _(o):
        plane_copy(o, lax.rem(xy + plane - o, plane)).wait_recv()
        twin_copy(o, core).start()

    @pl.loop(0, plane)
    def _(o):
        twin_copy(o, 1 - core).wait_recv()

    def apply_block(step, sums):
        lanes = pl.ds(pl.multiple_of(step * 512, 512), 512)
        block = z_full[:, lanes].astype(f32)
        waves = wv32[0:8, lanes]
        left = jnp.concatenate([block] + [block * waves[d:d + 1, :] for d in range(3)], axis=0).astype(bf16)
        return sums[0] + dot_nt(left, cos_a[:, lanes]), sums[1] + dot_nt(left, sin_a[:, lanes])

    blank = jnp.zeros((64, atoms), f32)
    by_cos, by_sin = lax.fori_loop(0, total_k // 512, apply_block, (blank, blank))
    pot_ref[...] = by_cos[:latent] + by_sin[latent:2 * latent]
    for d in range(3):
        first = 2 * latent * (d + 1)
        inner = by_sin[first:first + latent] - by_cos[first + latent:first + 2 * latent]
        force_ref[d:d + 1, :] = jnp.sum(charges * inner, axis=0, keepdims=True)

    for block in range(4):
        ghost_copy(block).wait_send()
        feat_copy(block).wait_send()
    spread_sent(pos_all, p_send, p_recv)
    spread_sent(q_all, q_send, q_recv)

    @pl.loop(1, depth)
    def _(o):
        column_copy(o).wait_send()

    @pl.loop(1, plane)
    def _(o):
        plane_copy(o, xy).wait_send()

    @pl.loop(0, plane)
    def _(o):
        twin_copy(o, core).wait_send()


def per_device(positions, species, neighbours, ghost_rows, wavevectors, embedding, w_in, radial, norm_gain, w_out, w_charge):
    atoms = positions.shape[1]
    total_k = wavevectors.shape[1]
    latent = w_charge.shape[1]
    channels = w_in.shape[2]
    bases = radial.shape[1]
    share = total_k // members
    scale = 1.0 / math.sqrt(atoms * lax.axis_size(("dom", "sub")))
    dma = pltpu.SemaphoreType.DMA
    vmem = pl.BlockSpec(memory_space=pltpu.VMEM)
    return pl.pallas_call(
        functools.partial(kernel, scale),
        out_shape=(
            jax.ShapeDtypeStruct((latent, atoms), f32),
            jax.ShapeDtypeStruct((3, atoms), f32),
        ),
        in_specs=[vmem] * 11,
        out_specs=(vmem, vmem),
        scratch_shapes=[
            pltpu.VMEM((16, atoms), f32),
            pltpu.VMEM((16, atoms), bf16),
            pltpu.VMEM((16, atoms), bf16),
            pltpu.VMEM((4, 16, atoms), bf16),
            pltpu.VMEM((8, atoms), f32),
            pltpu.VMEM((16, members * atoms), bf16),
            pltpu.VMEM((16, members * atoms), bf16),
            pltpu.VMEM((16, total_k), f32),
            pltpu.VMEM((16, total_k), bf16),
            pltpu.VMEM((share, 16), bf16),
            pltpu.VMEM((share, members * atoms), bf16),
            pltpu.VMEM((share, members * atoms), bf16),
            pltpu.VMEM((atoms, total_k), bf16),
            pltpu.VMEM((atoms, total_k), bf16),
            pltpu.VMEM((bases * atoms, 4 * atoms), bf16),
            pltpu.VMEM((atoms, channels), bf16),
            pltpu.VMEM((atoms, channels), bf16),
            pltpu.VMEM((16, share), bf16),
            pltpu.VMEM((depth, 16, share), bf16),
            pltpu.VMEM((16, total_k), bf16),
            dma((4,)), dma((4,)), dma((4,)), dma((4,)),
            dma((members,)), dma((members,)), dma((members,)), dma((members,)),
            dma((depth,)), dma((depth,)), dma((plane,)), dma((plane,)), dma((plane,)), dma((plane,)),
        ],
        compiler_params=pltpu.CompilerParams(
            collective_id=0, has_side_effects=True, vmem_limit_bytes=48 * 1024 * 1024
        ),
        name="ewald_step",
    )(
        positions, species.reshape(1, atoms), neighbours, ghost_rows, wavevectors,
        embedding, w_in, radial, norm_gain, w_out, w_charge,
    )


def solution(mesh):
    return jax.shard_map(
        per_device,
        mesh=mesh,
        in_specs=(
            P(None, ("dom", "sub")),
            P(("dom", "sub")),
            P(None, ("dom", "sub")),
            P(None, ("dom", "sub")),
            P(),
            P(),
            P(),
            P(),
            P(),
            P(),
            P(),
        ),
        out_specs=(P(None, ("dom", "sub")), P(None, ("dom", "sub"))),
        check_vma=False,
    )
```

time: 506 us -> 59.1 us (0.12)
  waiting for transfers between devices: 257 us -> 0 us
  local copies, waits for them, and re-layouts: 93.8 us -> 6.61 us
  other arithmetic: 68.2 us -> 0 us
  Pallas kernels: 0 us -> 51.5 us
  matrix products: 34.4 us -> 0 us
  starting transfers between devices: 34.4 us -> 0 us
  between operations: 14.3 us -> 0.71 us
    psum x1 -> x0, waiting for transfers between devices: 244 us -> none  [per_device(): weighted = lax.psum(structure, ('dom', 'sub')) * kweight[None, :]]
    gather x16 -> x0, local copies, waits for them, and re-layouts: 85.7 us -> none  [the longest x2 48 us: message_block(): gathered = feat_table[clamped].astype(jnp.float32)]
    pallas_call x0 -> x1, Pallas kernels: none -> 51.5 us  [per_device(): pl.pallas_call(functools.partial(kernel, scale), out_shape=(jax.ShapeDtyp...]
    cos x48 -> x0, other arithmetic: 49.8 us -> none  [phase_tile(): return (chosen, jnp.concatenate([jnp.cos(angle), jnp.sin(angle)], axis=0))]
    ppermute x12 -> x0, starting transfers between devices: 34.4 us -> none  [from_behind(): return lax.ppermute(value, axis, pairs)]
    dot_general x55 -> x0, matrix products: 34.4 us -> none  [the longest x24 13.1 us: accumulate(): lax.dot_general(charges, tile, (((1,), (1,)), ((), ())), precision=highes...]
    ppermute x12 -> x0, waiting for transfers between devices: 12.6 us -> none  [from_behind(): return lax.ppermute(value, axis, pairs)]
    reduce_sum x30 -> x0, other arithmetic: 9.39 us -> none  [the longest x2 7.31 us: message_block(): jnp.sum(jnp.where(live_mask, edge_weight * gathered, 0.0), axis=0)]
  transfers between devices with their start and end apart: 13 -> 0, of which waited for: 6 -> 0; matrix products, arithmetic and copies ran while one was open for 11% -> 0% of each run, Pallas kernels for 0% -> 0%
where the time goes in v1:
time: 59.1 us; the launch traced here: 58.8 us
  Pallas kernels  51.5 us (87%)
  local copies, waits for them, and re-layouts  6.61 us (11%)
  between operations  0.71 us (1%)
    pallas_call x1, Pallas kernels, per_device(): pl.pallas_call(functools.partial(kernel, scale), out_shape=(jax.ShapeDtyp...  51.5 us
    unnamed x23, local copies, waits for them, and re-layouts  6.61 us

profile of v1, /device:TPU:1, one launch (start us, length us, event | category | flops | bytes accessed | tf_op | source)
XLA Modules:
  0.0 58.8 jit_solution(6474320431401787652)
XLA Ops:
  0.6 0.0 copy-start.3
  0.6 0.0 copy-start.5
  0.7 0.0 copy-start.6
  0.7 0.0 copy-start.7
  0.7 0.8 %copy.13.wch_ref = bf16[128,8]{1,0:T(8,128)(2,1)S(1)} copy(bf16[128,8]{0,1:T(8,128)(2,1)} %param.21) | data formatting | bytes 4096 | tf_op args[10]
  1.5 0.0 copy-done.3
  1.5 0.0 copy-done.5
  1.5 0.0 copy-done.6
  1.5 0.0 copy-done.7
  1.5 0.0 copy-start
  1.5 0.9 %copy-done = s32[3,12288]{1,0:T(4,128)S(1)} copy-done((s32[3,12288]{1,0:T(4,128)S(1)}, s32[3,12288]{1,0:T(4,128)}, u32[]{:S(2)}) %copy-start) | copy-done | bytes 147480
  2.5 0.0 copy-start.1
  2.5 0.8 %copy-done.1 = bf16[2,128,128]{2,1,0:T(8,128)(2,1)S(1)} copy-done((bf16[2,128,128]{2,1,0:T(8,128)(2,1)S(1)}, bf16[2,128,128]{2,1,0:T(8,128)(2,1)}, u32[]{:S(2)}) %copy-start.1) | copy-done | bytes 65560
  3.3 0.0 copy-start.2
  3.3 0.8 %copy-done.2 = bf16[2,128,128]{2,1,0:T(8,128)(2,1)S(1)} copy-done((bf16[2,128,128]{2,1,0:T(8,128)(2,1)S(1)}, bf16[2,128,128]{2,1,0:T(8,128)(2,1)}, u32[]{:S(2)}) %copy-start.2) | copy-done | bytes 65560
  4.1 0.0 copy-start.4
  4.1 0.7 %copy-done.4 = bf16[2,8,128]{2,1,0:T(8,128)(2,1)S(1)} copy-done((bf16[2,8,128]{2,1,0:T(8,128)(2,1)S(1)}, bf16[2,8,128]{2,1,0:T(8,128)(2,1)}, u32[]{:S(2)}) %copy-start.4) | copy-done | bytes 4120
  4.8 0.0 copy-start.8
  4.8 0.7 %copy-done.8 = bf16[2,128]{1,0:T(2,128)(2,1)S(1)} copy-done((bf16[2,128]{1,0:T(2,128)(2,1)S(1)}, bf16[2,128]{1,0:T(2,128)(2,1)}, u32[]{:S(2)}) %copy-start.8) | copy-done | bytes 536
  5.5 0.0 copy-start.9
  5.5 0.7 %copy-done.9 = bf16[2,128]{1,0:T(2,128)(2,1)S(1)} copy-done((bf16[2,128]{1,0:T(2,128)(2,1)S(1)}, bf16[2,128]{1,0:T(2,128)(2,1)}, u32[]{:S(2)}) %copy-start.9) | copy-done | bytes 536
  6.1 51.5 %ewald_step.1 = (f32[8,128]{1,0:T(8,128)S(1)}, f32[3,128]{1,0:T(4,128)S(1)}) custom-call(bf16[3,128]{1,0:T(4,128)(2,1)S(1)} %copy-done.6, s32[1,128]{1,0:T(1,128)S(1)} %bitcast.1, s32[64,128]{1,0:T(8,128)S(1)} %copy-done.3, s32[4,32]{1,0:T(4,128)S(1)} %copy-done.5, s32[3,12288]{1,0:T(4,128)S(1)} %copy-done, bf16[2,128]{1,0:T(2,128)(2,1)S(1)} %copy-done.8, ...), custom_call_target="tpu_custom_call" | custom-call | tf_op jit(solution)/shard_map/ewald_step/pallas_call | solution.py:375
  57.6 0.6 %copy.16 = f32[8,128]{1,0:T(8,128)} copy(f32[8,128]{1,0:T(8,128)S(1)} %get-tuple-element.4) | data formatting | bytes 8192
  58.2 0.6 copy.17
Async XLA Ops:
  0.6 0.9 %copy-start.3 = (s32[64,128]{1,0:T(8,128)S(1)}, s32[64,128]{1,0:T(8,128)}, u32[]{:S(2)}) copy-start(s32[64,128]{1,0:T(8,128)} %nbr_ref.1) | copy-start | bytes 98308
  0.6 0.9 %copy-start.5 = (s32[4,32]{1,0:T(4,128)S(1)}, s32[4,32]{1,0:T(4,128)}, u32[]{:S(2)}) copy-start(s32[4,32]{1,0:T(4,128)} %gr_ref.1) | copy-start | bytes 1540
  0.7 0.9 %copy-start.6 = (bf16[3,128]{1,0:T(4,128)(2,1)S(1)}, bf16[3,128]{1,0:T(4,128)(2,1)}, u32[]{:S(2)}) copy-start(bf16[3,128]{1,0:T(4,128)(2,1)} %pos_ref.1) | copy-start | bytes 2308
  0.7 0.9 %copy-start.7 = (s32[128]{0:T(128)S(1)}, s32[128]{0:T(128)}, u32[]{:S(2)}) copy-start(s32[128]{0:T(128)} %param.12) | copy-start | bytes 1540
  1.5 0.9 %copy-start = (s32[3,12288]{1,0:T(4,128)S(1)}, s32[3,12288]{1,0:T(4,128)}, u32[]{:S(2)}) copy-start(s32[3,12288]{1,0:T(4,128)} %wv_ref.1) | copy-start | bytes 442372
  2.5 0.8 %copy-start.1 = (bf16[2,128,128]{2,1,0:T(8,128)(2,1)S(1)}, bf16[2,128,128]{2,1,0:T(8,128)(2,1)}, u32[]{:S(2)}) copy-start(bf16[2,128,128]{2,1,0:T(8,128)(2,1)} %win_ref.1) | copy-start | bytes 196612
  3.3 0.8 %copy-start.2 = (bf16[2,128,128]{2,1,0:T(8,128)(2,1)S(1)}, bf16[2,128,128]{2,1,0:T(8,128)(2,1)}, u32[]{:S(2)}) copy-start(bf16[2,128,128]{2,1,0:T(8,128)(2,1)} %wout_ref.1) | copy-start | bytes 196612
  4.1 0.7 %copy-start.4 = (bf16[2,8,128]{2,1,0:T(8,128)(2,1)S(1)}, bf16[2,8,128]{2,1,0:T(8,128)(2,1)}, u32[]{:S(2)}) copy-start(bf16[2,8,128]{2,1,0:T(8,128)(2,1)} %rad_ref.1) | copy-start | bytes 12292
  4.8 0.7 %copy-start.8 = (bf16[2,128]{1,0:T(2,128)(2,1)S(1)}, bf16[2,128]{1,0:T(2,128)(2,1)}, u32[]{:S(2)}) copy-start(bf16[2,128]{1,0:T(2,128)(2,1)} %emb_ref.1) | copy-start | bytes 1540
  5.5 0.7 %copy-start.9 = (bf16[2,128]{1,0:T(2,128)(2,1)S(1)}, bf16[2,128]{1,0:T(2,128)(2,1)}, u32[]{:S(2)}) copy-start(bf16[2,128]{1,0:T(2,128)(2,1)} %gain_ref.1) | copy-start | bytes 1540

commit v2 on v1

v2 whole, which is shorter than its diff:
```python
import functools
import math

import jax
import jax.numpy as jnp
import numpy as np
from jax import lax
from jax.experimental import pallas as pl
from jax.experimental.pallas import tpu as pltpu
from jax.sharding import PartitionSpec as P

MESH = pl.DeviceIdType.MESH
smearing = 0.005
epsilon = 1e-05
f32 = jnp.float32
bf16 = jnp.bfloat16
side = 4
plane = side * side
members = 2 * plane
depth = 8
round_magic = 12582912.0


def fit_series(function, terms):
    nodes = (np.cos(np.pi * (np.arange(4 * terms) + 0.5) / (4 * terms)) + 1.0) / 8.0
    fitted = np.polynomial.chebyshev.Chebyshev.fit(nodes, function(np.sqrt(nodes)), terms - 1, domain=[0.0, 0.25])
    return [float(c) for c in fitted.convert(kind=np.polynomial.Polynomial).coef]


def cos_series(terms):
    return fit_series(lambda t: np.cos(2.0 * np.pi * t), terms)


def sin_series(terms):
    return fit_series(lambda t: np.sin(2.0 * np.pi * t) / t, terms)


def horner(coefs, u):
    value = coefs[-1]
    for c in coefs[-2::-1]:
        value = value * u + c
    return value


def turns_cos_sin(turns, cos_coefs, sin_coefs):
    t = turns - ((turns + round_magic) - round_magic)
    u = t * t
    return horner(cos_coefs, u), t * horner(sin_coefs, u)


def dot_nt(a, b):
    return lax.dot_general(a, b, (((1,), (1,)), ((), ())), preferred_element_type=f32)


def dot_nn(a, b):
    return jnp.dot(a, b, preferred_element_type=f32)


def torus_offsets():
    every = [(dx, dy, dc) for dx in range(side) for dy in range(side) for dc in range(2)]
    return sorted(every, key=lambda o: (min(o[0], side - o[0]) + min(o[1], side - o[1]), o))


def opposite(offset):
    return (-offset[0] % side, -offset[1] % side, offset[2])


def kernel(
    scale,
    pos_hbm, spec_hbm, gr_hbm, nbr_hbm, wv_hbm, emb_hbm, win_hbm, rad_hbm, gain_hbm, wout_hbm, wch_hbm,
    out_ref,
    pos_ref, spec_ref, gr_ref, nbr_ref, wv_ref, emb_ref, win_ref, rad_ref, gain_ref, wout_ref, wch_ref,
    c32, coords, ghost_out, ghost_in, gpad, pos_all, q_all, wv32, share_waves,
    share_phase, atom_phase, pairs_own, pairs_ghost, feat_out, feat_in, z_out, z_in, z_full, left,
    in_sem, g1_send, g1_recv, g2_send, g2_recv, p_send, p_recv, q_send, q_recv,
    zs_send, zs_recv, w_send, w_recv, x_send, x_recv,
):
    dom = lax.axis_index("dom")
    sub = lax.axis_index("sub")
    n_dom = lax.axis_size("dom")
    n_sub = lax.axis_size("sub")
    zl, xy = dom // plane, lax.rem(dom, plane)
    my_x, my_y = xy // side, lax.rem(xy, side)
    zh, core = sub // 2, lax.rem(sub, 2)
    z_me = zh * (depth // 2) + zl
    atoms = pos_ref.shape[1]
    total_k = wv_ref.shape[1]
    share = total_k // members
    half_k = total_k // 2
    latent = wch_ref.shape[0]
    bases = rad_ref.shape[1]
    ghosts = gr_ref.shape[1]

    def member(offset):
        dx, dy, dc = offset
        chip = lax.rem(my_x + dx, side) * side + lax.rem(my_y + dy, side)
        return (zl * plane + chip, zh * 2 + (1 - core if dc else core))

    def column_member(dz):
        index = lax.rem(z_me + dz, depth)
        return (lax.rem(index, depth // 2) * plane + xy, (index // (depth // 2)) * 2 + core)

    neighbours_at = (
        (lax.rem(dom + 1, n_dom), sub),
        (lax.rem(dom + n_dom - 1, n_dom), sub),
        (dom, lax.rem(sub + 1, n_sub)),
        (dom, lax.rem(sub + n_sub - 1, n_sub)),
    )
    offsets = torus_offsets()
    slot_of = {offset: slot for slot, offset in enumerate(offsets)}
    chip_offsets = [offset for offset in offsets if offset[2] == 0]
    heights = sorted(range(1, depth), key=lambda dz: -min(dz, depth - dz))

    fetches = [
        pltpu.make_async_copy(source, target, in_sem.at[number])
        for number, (source, target) in enumerate((
            (pos_hbm, pos_ref), (spec_hbm, spec_ref), (gr_hbm, gr_ref), (nbr_hbm, nbr_ref), (wv_hbm, wv_ref),
            (emb_hbm, emb_ref), (win_hbm, win_ref), (rad_hbm, rad_ref), (gain_hbm, gain_ref), (wout_hbm, wout_ref),
            (wch_hbm, wch_ref)))
    ]
    barrier = pltpu.get_barrier_semaphore()

    def greet(target):
        pl.semaphore_signal(barrier, inc=1, device_id=target, device_id_type=MESH)

    for target in neighbours_at[::-1]:
        greet(target)
    for fetch in fetches[:3]:
        fetch.start()
    for offset in offsets[:0:-1]:
        greet(member(offset))
    for dz in heights:
        greet(column_member(dz))
    for fetch in fetches[3:]:
        fetch.start()

    c32[...] = jnp.zeros_like(c32)
    gpad[...] = jnp.zeros_like(gpad)
    for fetch in fetches[:3]:
        fetch.wait()
    c32[0:3, :] = pos_ref[...].astype(f32)
    c32[3:4, :] = spec_ref[...].astype(f32)
    own32 = c32[...]
    coords[...] = own32.astype(bf16)
    gpad[0:4, 0:ghosts] = gr_ref[...].astype(f32)
    grown = gpad[...]
    picks = grown[1:2, :]
    for block, source in ((1, 0), (2, 3), (3, 2)):
        picks = picks + pltpu.roll(grown, block * ghosts, axis=1)[source:source + 1, :]
    row_number = lax.broadcasted_iota(jnp.int32, (atoms, atoms), 0).astype(f32)
    pick_cols = jnp.where(row_number == picks, 1.0, 0.0)
    ghost_out[...] = dot_nn(own32.astype(bf16), pick_cols.astype(bf16)).astype(bf16)
    pos_all[:, 0:atoms] = own32.astype(bf16)

    def ghost_copy(block):
        return pltpu.make_async_remote_copy(
            src_ref=ghost_out, dst_ref=ghost_in.at[block], send_sem=g1_send, recv_sem=g1_recv,
            device_id=neighbours_at[block], device_id_type=MESH)

    def feat_copy(block):
        rows = pl.ds(block * ghosts, ghosts)
        return pltpu.make_async_remote_copy(
            src_ref=feat_out.at[rows], dst_ref=feat_in.at[rows], send_sem=g2_send, recv_sem=g2_recv,
            device_id=neighbours_at[block], device_id_type=MESH)

    def slot_lanes(first, count):
        return pl.ds(first * atoms, count * atoms)

    near_count = members // 2

    def spread_copy(buffer, send, recv, offset):
        landing = slot_of[opposite(offset)]
        return pltpu.make_async_remote_copy(
            src_ref=buffer.at[:, slot_lanes(0, 1)], dst_ref=buffer.at[:, slot_lanes(landing, 1)],
            send_sem=send, recv_sem=recv.at[0 if landing < near_count else 1],
            device_id=member(offset), device_id_type=MESH)

    def spread_all(buffer, send, recv, first, count, group):
        lanes = slot_lanes(first, count)
        return pltpu.make_async_remote_copy(
            src_ref=buffer.at[:, lanes], dst_ref=buffer.at[:, lanes], send_sem=send, recv_sem=recv.at[group],
            device_id=member(offsets[1]), device_id_type=MESH)

    def spread_start(buffer, send, recv):
        for offset in offsets[:0:-1]:
            spread_copy(buffer, send, recv, offset).start()

    def spread_near(buffer, send, recv):
        spread_all(buffer, send, recv, 1, near_count - 1, 0).wait_recv()

    def spread_far(buffer, send, recv):
        spread_all(buffer, send, recv, near_count, members - near_count, 1).wait_recv()

    def spread_sent(buffer, send, recv):
        spread_all(buffer, send, recv, 1, members - 1, 0).wait_send()

    def column_copy(dz):
        return pltpu.make_async_remote_copy(
            src_ref=z_out, dst_ref=z_in.at[dz - 1], send_sem=zs_send, recv_sem=zs_recv,
            device_id=column_member(dz), device_id_type=MESH)

    column_all = pltpu.make_async_remote_copy(
        src_ref=z_in, dst_ref=z_in, send_sem=zs_send, recv_sem=zs_recv,
        device_id=column_member(1), device_id_type=MESH)

    def chip_share(offset, which_core):
        chip = lax.rem(my_x + offset[0], side) * side + lax.rem(my_y + offset[1], side)
        return pl.ds(pl.multiple_of((which_core * plane + chip) * share, 128), share)

    def plane_copy(number, owner):
        lanes = chip_share(owner, core)
        return pltpu.make_async_remote_copy(
            src_ref=z_full.at[:, lanes], dst_ref=z_full.at[:, lanes], send_sem=w_send, recv_sem=w_recv.at[number],
            device_id=member(chip_offsets[number]), device_id_type=MESH)

    plane_all = pltpu.make_async_remote_copy(
        src_ref=z_full.at[:, pl.ds(0, (plane - 1) * share)], dst_ref=z_full.at[:, pl.ds(0, (plane - 1) * share)],
        send_sem=w_send, recv_sem=w_recv.at[0], device_id=member(chip_offsets[1]), device_id_type=MESH)
    twin = (dom, zh * 2 + 1 - core)

    def twin_copy(offset):
        lanes = chip_share(offset, core)
        return pltpu.make_async_remote_copy(
            src_ref=z_full.at[:, lanes], dst_ref=z_full.at[:, lanes], send_sem=x_send, recv_sem=x_recv,
            device_id=twin, device_id_type=MESH)

    twin_all = pltpu.make_async_remote_copy(
        src_ref=z_full.at[:, pl.ds(0, half_k)], dst_ref=z_full.at[:, pl.ds(0, half_k)],
        send_sem=x_send, recv_sem=x_recv, device_id=twin, device_id_type=MESH)
    ghost_all = pltpu.make_async_remote_copy(
        src_ref=ghost_in, dst_ref=ghost_in, send_sem=g1_send, recv_sem=g1_recv, device_id=twin, device_id_type=MESH)
    feat_all = pltpu.make_async_remote_copy(
        src_ref=feat_in, dst_ref=feat_in, send_sem=g2_send, recv_sem=g2_recv, device_id=twin, device_id_type=MESH)

    pl.semaphore_wait(barrier, 4 + (members - 1) + (depth - 1))
    for block in (3, 2, 1, 0):
        ghost_copy(block).start()
    spread_start(pos_all, p_send, p_recv)

    for fetch in fetches[3:]:
        fetch.wait()
    listed = nbr_ref[...]
    quarters = []
    for first in range(0, 2 * atoms, 64):
        table_row = lax.broadcasted_iota(jnp.int32, (64, atoms), 0) + first
        counted = jnp.zeros((64, atoms), f32)
        for slot in range(listed.shape[0]):
            counted = jnp.where(table_row == listed[slot:slot + 1, :], counted + 1.0, counted)
        quarters.append(counted)
    own_counts = jnp.concatenate(quarters[:2], axis=0).T
    ghost_counts = jnp.concatenate(quarters[2:], axis=0).T
    pick_rows = pick_cols.T.astype(bf16)

    cos_fine, sin_fine = cos_series(9), sin_series(9)
    cos_fast, sin_fast = cos_series(6), sin_series(5)
    own_cos, own_sin = turns_cos_sin(0.5 * own32, cos_fine, sin_fine)
    own_cos_col, own_sin_col = own_cos.T, own_sin.T
    embedding = emb_ref[...].astype(f32)
    gains = gain_ref[...].astype(f32)
    is_second = own32.T[:, 3:4] > 0.5
    hidden = jnp.where(is_second, embedding[1:2, :], embedding[0:1, :])
    both = lax.broadcasted_iota(jnp.int32, (16, embedding.shape[1]), 0)
    both = jnp.where(both == 1, embedding[1:2, :], embedding[0:1, :]).astype(bf16)
    projected_kinds = dot_nn(both, win_ref[0]).astype(bf16).astype(f32)
    own_feats = jnp.where(is_second, projected_kinds[1:2, :], projected_kinds[0:1, :]).astype(bf16)

    def fill_pairs(pairs, counts, table_cos, table_sin):
        chord = jnp.zeros((atoms, atoms), f32)
        for d in range(3):
            apart = table_sin[d:d + 1, :] * own_cos_col[:, d:d + 1] - table_cos[d:d + 1, :] * own_sin_col[:, d:d + 1]
            chord = chord + apart * apart
        basis = jnp.exp(-0.125 * chord)
        for b in range(bases):
            pair = counts * basis
            high = pair.astype(bf16)
            rows = slice(b * atoms, (b + 1) * atoms)
            pairs[rows, 0:atoms] = high
            pairs[rows, atoms:2 * atoms] = (pair - high.astype(f32)).astype(bf16)
            basis = basis * basis

    def messages(number, pairs, feats):
        products = dot_nn(pairs[...], jnp.concatenate([feats, feats], axis=0))
        radial_layer = rad_ref[number].astype(f32)
        message = radial_layer[0:1, :] * products[:atoms]
        for b in range(1, bases):
            message = message + radial_layer[b:b + 1, :] * products[b * atoms:(b + 1) * atoms]
        return message

    def update(number, hidden, message):
        normed = message * lax.rsqrt(jnp.mean(message * message, axis=1, keepdims=True) + epsilon)
        normed = normed * gains[number:number + 1, :]
        activated = (normed / (1.0 + jnp.exp(-normed))).astype(bf16)
        return (hidden + dot_nn(activated, wout_ref[number])).astype(bf16)

    fill_pairs(pairs_own, own_counts, own_cos, own_sin)
    own_message = messages(0, pairs_own, own_feats)

    wv32[...] = jnp.zeros_like(wv32)
    wv32[0:3, :] = wv_ref[...].astype(f32)
    own_waves = wv32[:, chip_share((0, 0), core)]
    share_waves[0:8, :] = own_waves
    share_waves[8:16, :] = jnp.zeros_like(own_waves)
    squared = jnp.sum(own_waves * own_waves, axis=0, keepdims=True)
    kweight = jnp.exp(-smearing * squared) / squared * scale

    ghost_all.wait_recv()
    lane_block = lax.broadcasted_iota(jnp.int32, (16, atoms), 1) // ghosts
    ghost32 = jnp.zeros((16, atoms), f32)
    for block in range(4):
        ghost32 = jnp.where(lane_block == block, ghost_in[block].astype(f32), ghost32)
    ghost_cos, ghost_sin = turns_cos_sin(0.5 * ghost32, cos_fine, sin_fine)
    fill_pairs(pairs_ghost, ghost_counts, ghost_cos, ghost_sin)
    ghost_second = ghost32.T[:, 3:4] > 0.5
    ghost_feats = jnp.where(ghost_second, projected_kinds[1:2, :], projected_kinds[0:1, :]).astype(bf16)
    hidden = update(0, hidden, own_message + messages(0, pairs_ghost, ghost_feats))
    projected = dot_nn(hidden, win_ref[1]).astype(bf16)
    feat_out[...] = dot_nn(pick_rows, projected).astype(bf16)
    for block in (3, 2, 1, 0):
        feat_copy(block).start()
    own_message = messages(1, pairs_own, projected)

    spread_near(pos_all, p_send, p_recv)
    spread_far(pos_all, p_send, p_recv)
    waves16 = share_waves[...].astype(bf16)

    def share_phases(step):
        for part in range(4):
            rows = pl.ds(pl.multiple_of(step * 512 + part * 128, 128), 128)
            places = pos_all[:, rows].astype(f32).T.astype(bf16)
            cosines, sines = turns_cos_sin(dot_nn(places, waves16), cos_fast, sin_fast)
            share_phase[rows, 0:share] = cosines.astype(bf16)
            share_phase[rows, share:2 * share] = sines.astype(bf16)

    def atom_phases(step):
        for part in range(8):
            rows = pl.ds(pl.multiple_of(step * 2048 + part * 256, 256), 256)
            waves = wv32[:, rows].T
            waves = jnp.concatenate([waves, jnp.zeros_like(waves)], axis=1).astype(bf16)
            cosines, sines = turns_cos_sin(dot_nn(waves, coords[...]), cos_fast, sin_fast)
            atom_phase[rows, 0:atoms] = cosines.astype(bf16)
            atom_phase[rows, atoms:2 * atoms] = sines.astype(bf16)

    share_steps = members * atoms // 512
    atom_steps = total_k // 2048
    pl.loop(0, share_steps)(share_phases)
    ghost_all.wait_send()
    spread_sent(pos_all, p_send, p_recv)

    feat_all.wait_recv()
    hidden = update(1, hidden, own_message + messages(1, pairs_ghost, feat_in[...]))
    charges = dot_nt(wch_ref[...], hidden)
    charges_high = charges.astype(bf16).astype(f32)
    q_all[:, 0:atoms] = jnp.concatenate([charges_high, charges - charges_high], axis=0).astype(bf16)
    spread_start(q_all, q_send, q_recv)
    pl.loop(0, atom_steps // 2)(atom_phases)
    feat_all.wait_send()

    near_lanes, far_lanes = slice(0, near_count * atoms), slice(near_count * atoms, members * atoms)
    spread_near(q_all, q_send, q_recv)
    both_parts = dot_nn(q_all[:, near_lanes], share_phase[near_lanes, :])
    spread_far(q_all, q_send, q_recv)
    both_parts = both_parts + dot_nn(q_all[:, far_lanes], share_phase[far_lanes, :])
    both_parts = both_parts[:latent] + both_parts[latent:]
    z_out[...] = (jnp.concatenate([both_parts[:, :share], both_parts[:, share:]], axis=0) * kweight).astype(bf16)
    for dz in heights:
        column_copy(dz).start()
    pl.loop(atom_steps // 2, atom_steps)(atom_phases)
    spread_sent(q_all, q_send, q_recv)

    column_all.wait_recv()
    summed = z_out[...].astype(f32)
    for dz in range(1, depth):
        summed = summed + z_in[dz - 1].astype(f32)
    z_full[:, chip_share((0, 0), core)] = summed.astype(bf16)
    for number in range(plane - 1, 0, -1):
        plane_copy(number, (0, 0)).start()
    twin_copy((0, 0)).start()
    column_all.wait_send()
    for number in range(1, plane):
        source = opposite(chip_offsets[number])
        plane_copy(number, source).wait_recv()
        twin_copy(source).start()
    plane_all.wait_send()

    def apply_half(which_core):
        start = pl.multiple_of(which_core * half_k, half_k)
        for first in range(0, half_k, 512):
            lanes = pl.ds(pl.multiple_of(start + first, 512), 512)
            block = z_full[:, lanes].astype(f32)
            waves = wv32[:, lanes]
            here = slice(first, first + 512)
            left[0:16, here] = z_full[:, lanes]
            for d in range(3):
                left[16 * (d + 1):16 * (d + 2), here] = (block * waves[d:d + 1, :]).astype(bf16)
        return dot_nn(left[...], atom_phase[pl.ds(start, half_k), :])

    sums = apply_half(core)
    twin_all.wait_recv()
    sums = sums + apply_half(1 - core)
    by_cos, by_sin = sums[:, :atoms], sums[:, atoms:]
    out_ref[...] = jnp.zeros_like(out_ref)
    out_ref[0:latent, :] = by_cos[:latent] + by_sin[latent:2 * latent]
    for d in range(3):
        first = 2 * latent * (d + 1)
        inner = by_sin[first:first + latent] - by_cos[first + latent:first + 2 * latent]
        out_ref[latent + d:latent + d + 1, :] = jnp.sum(charges * inner, axis=0, keepdims=True)
    twin_all.wait_send()


def per_device(positions, species, neighbours, ghost_rows, wavevectors, embedding, w_in, radial, norm_gain, w_out, w_charge):
    atoms = positions.shape[1]
    total_k = wavevectors.shape[1]
    latent = w_charge.shape[1]
    channels = w_in.shape[2]
    bases = radial.shape[1]
    share = total_k // members
    scale = 1.0 / math.sqrt(atoms * lax.axis_size(("dom", "sub")))
    operands = (
        positions, species.reshape(1, atoms), ghost_rows, neighbours, wavevectors,
        embedding, w_in, radial, norm_gain, w_out, w_charge.T,
    )
    dma = pltpu.SemaphoreType.DMA
    vmem = pl.BlockSpec(memory_space=pltpu.VMEM)
    hbm = pl.BlockSpec(memory_space=pltpu.HBM)
    packed = pl.pallas_call(
        functools.partial(kernel, scale),
        out_shape=jax.ShapeDtypeStruct((16, atoms), f32),
        in_specs=[hbm] * len(operands),
        out_specs=vmem,
        scratch_shapes=[pltpu.VMEM(value.shape, value.dtype) for value in operands] + [
            pltpu.VMEM((16, atoms), f32),
            pltpu.VMEM((16, atoms), bf16),
            pltpu.VMEM((16, atoms), bf16),
            pltpu.VMEM((4, 16, atoms), bf16),
            pltpu.VMEM((8, atoms), f32),
            pltpu.VMEM((16, members * atoms), bf16),
            pltpu.VMEM((16, members * atoms), bf16),
            pltpu.VMEM((8, total_k), f32),
            pltpu.VMEM((16, share), f32),
            pltpu.VMEM((members * atoms, 2 * share), bf16),
            pltpu.VMEM((total_k, 2 * atoms), bf16),
            pltpu.VMEM((bases * atoms, 2 * atoms), bf16),
            pltpu.VMEM((bases * atoms, 2 * atoms), bf16),
            pltpu.VMEM((atoms, channels), bf16),
            pltpu.VMEM((atoms, channels), bf16),
            pltpu.VMEM((16, share), bf16),
            pltpu.VMEM((depth - 1, 16, share), bf16),
            pltpu.VMEM((16, total_k), bf16),
            pltpu.VMEM((64, total_k // 2), bf16),
            dma((len(operands),)), dma, dma, dma, dma, dma, dma((2,)), dma, dma((2,)),
            dma, dma, dma, dma((plane,)), dma, dma,
        ],
        compiler_params=pltpu.CompilerParams(
            collective_id=0, has_side_effects=True, vmem_limit_bytes=60 * 1024 * 1024
        ),
        name="ewald_step",
    )(*operands)
    return packed[:latent], packed[latent:latent + 3]


def solution(mesh):
    return jax.shard_map(
        per_device,
        mesh=mesh,
        in_specs=(
            P(None, ("dom", "sub")),
            P(("dom", "sub")),
            P(None, ("dom", "sub")),
            P(None, ("dom", "sub")),
            P(),
            P(),
            P(),
            P(),
            P(),
            P(),
            P(),
        ),
        out_specs=(P(None, ("dom", "sub")), P(None, ("dom", "sub"))),
        check_vma=False,
    )
```

time: 59.1 us -> 47.2 us (0.80)
  Pallas kernels: 51.5 us -> 43.8 us
  local copies, waits for them, and re-layouts: 6.61 us -> 2.53 us
    pallas_call x1, Pallas kernels: 51.5 us -> 43.8 us  [per_device(): pl.pallas_call(functools.partial(kernel, scale), out_shape=jax.ShapeDtype...]
    unnamed x23 -> x0, local copies, waits for them, and re-layouts: 6.61 us -> none
    slice x0 -> x2, local copies, waits for them, and re-layouts: none -> 2.53 us  [per_device(): return (packed[:latent], packed[latent:latent + 3])]
where the time goes in v2:
time: 47.2 us; the launch traced here: 47 us
  Pallas kernels  43.8 us (93%)
  local copies, waits for them, and re-layouts  2.53 us (5%)
  between operations  0.64 us (1%)
    pallas_call x1, Pallas kernels, per_device(): pl.pallas_call(functools.partial(kernel, scale), out_shape=jax.ShapeDtype...  43.8 us
    slice x2, local copies, waits for them, and re-layouts, per_device(): return (packed[:latent], packed[latent:latent + 3])  2.53 us

profile of v2, /device:TPU:1, one launch (start us, length us, event | category | flops | bytes accessed | tf_op | source)
XLA Modules:
  0.0 47.0 jit_solution(17564178401791944734)
XLA Ops:
  0.6 43.8 %ewald_step.1 = f32[16,128]{1,0:T(8,128)} custom-call(bf16[3,128]{1,0:T(4,128)(2,1)} %pos_hbm.1, s32[1,128]{1,0:T(1,128)} %bitcast.3, s32[4,32]{1,0:T(4,128)} %gr_hbm.1, s32[64,128]{1,0:T(8,128)} %nbr_hbm.1, s32[3,12288]{1,0:T(4,128)} %wv_hbm.1, bf16[2,128]{1,0:T(2,128)(2,1)} %emb_hbm.1, bf16[2,128,128]{2,1,0:T(8,128)(2,1)} %win_hbm.1, ...), custom_call_target="tpu_custom_call" | custom-call | tf_op jit(solution)/shard_map/ewald_step/pallas_call | solution.py:425
  44.5 1.3 %slice.7 = f32[3,128]{1,0:T(4,128)} slice(f32[16,128]{1,0:T(8,128)} %ewald_step.1), slice={[8:11], [0:128]} | slice | bytes 3072 | tf_op jit(solution)/shard_map/slice | solution.py:458
  45.7 1.3 %slice.6 = f32[8,128]{1,0:T(8,128)} slice(f32[16,128]{1,0:T(8,128)} %ewald_step.1), slice={[0:8], [0:128]} | slice | bytes 8192 | tf_op jit(solution)/shard_map/slice | solution.py:458

commit v3 on v2

--- a/solution.py
+++ b/solution.py
@@ -70,7 +70,7 @@
     pos_hbm, spec_hbm, gr_hbm, nbr_hbm, wv_hbm, emb_hbm, win_hbm, rad_hbm, gain_hbm, wout_hbm, wch_hbm,
     out_ref,
     pos_ref, spec_ref, gr_ref, nbr_ref, wv_ref, emb_ref, win_ref, rad_ref, gain_ref, wout_ref, wch_ref,
-    c32, coords, ghost_out, ghost_in, gpad, pos_all, q_all, wv32, share_waves,
+    c32, ghost_out, ghost_in, gpad, pos_all, q_all, wv32,
     share_phase, atom_phase, pairs_own, pairs_ghost, feat_out, feat_in, z_out, z_in, z_full, left,
     in_sem, g1_send, g1_recv, g2_send, g2_recv, p_send, p_recv, q_send, q_recv,
     zs_send, zs_recv, w_send, w_recv, x_send, x_recv,
@@ -86,7 +86,6 @@
     atoms = pos_ref.shape[1]
     total_k = wv_ref.shape[1]
     share = total_k // members
-    half_k = total_k // 2
     latent = wch_ref.shape[0]
     bases = rad_ref.shape[1]
     ghosts = gr_ref.shape[1]
@@ -141,7 +140,7 @@
     c32[0:3, :] = pos_ref[...].astype(f32)
     c32[3:4, :] = spec_ref[...].astype(f32)
     own32 = c32[...]
-    coords[...] = own32.astype(bf16)
+    own_coords = own32.astype(bf16)
     gpad[0:4, 0:ghosts] = gr_ref[...].astype(f32)
     grown = gpad[...]
     picks = grown[1:2, :]
@@ -149,8 +148,8 @@
         picks = picks + pltpu.roll(grown, block * ghosts, axis=1)[source:source + 1, :]
     row_number = lax.broadcasted_iota(jnp.int32, (atoms, atoms), 0).astype(f32)
     pick_cols = jnp.where(row_number == picks, 1.0, 0.0)
-    ghost_out[...] = dot_nn(own32.astype(bf16), pick_cols.astype(bf16)).astype(bf16)
-    pos_all[:, 0:atoms] = own32.astype(bf16)
+    ghost_out[...] = dot_nn(own_coords, pick_cols.astype(bf16)).astype(bf16)
+    pos_all[:, 0:atoms] = own_coords
 
     def ghost_copy(block):
         return pltpu.make_async_remote_copy(
@@ -203,30 +202,43 @@
         src_ref=z_in, dst_ref=z_in, send_sem=zs_send, recv_sem=zs_recv,
         device_id=column_member(1), device_id_type=MESH)
 
-    def chip_share(offset, which_core):
-        chip = lax.rem(my_x + offset[0], side) * side + lax.rem(my_y + offset[1], side)
-        return pl.ds(pl.multiple_of((which_core * plane + chip) * share, 128), share)
-
-    def plane_copy(number, owner):
-        lanes = chip_share(owner, core)
-        return pltpu.make_async_remote_copy(
-            src_ref=z_full.at[:, lanes], dst_ref=z_full.at[:, lanes], send_sem=w_send, recv_sem=w_recv.at[number],
-            device_id=member(chip_offsets[number]), device_id_type=MESH)
+    def share_lanes(first, count):
+        return pl.ds(first * share, count * share)
+
+    def plane_copy(number):
+        landing = chip_offsets.index(opposite(chip_offsets[number]))
+        return pltpu.make_async_remote_copy(
+            src_ref=z_full.at[:, share_lanes(0, 1)], dst_ref=z_full.at[:, share_lanes(landing, 1)],
+            send_sem=w_send, recv_sem=w_recv.at[landing], device_id=member(chip_offsets[number]), device_id_type=MESH)
+
+    def plane_arrival(slot):
+        lanes = share_lanes(slot, 1)
+        return pltpu.make_async_remote_copy(
+            src_ref=z_full.at[:, lanes], dst_ref=z_full.at[:, lanes], send_sem=w_send, recv_sem=w_recv.at[slot],
+            device_id=member(chip_offsets[1]), device_id_type=MESH)
 
     plane_all = pltpu.make_async_remote_copy(
-        src_ref=z_full.at[:, pl.ds(0, (plane - 1) * share)], dst_ref=z_full.at[:, pl.ds(0, (plane - 1) * share)],
+        src_ref=z_full.at[:, share_lanes(1, plane - 1)], dst_ref=z_full.at[:, share_lanes(1, plane - 1)],
         send_sem=w_send, recv_sem=w_recv.at[0], device_id=member(chip_offsets[1]), device_id_type=MESH)
     twin = (dom, zh * 2 + 1 - core)
-
-    def twin_copy(offset):
-        lanes = chip_share(offset, core)
-        return pltpu.make_async_remote_copy(
-            src_ref=z_full.at[:, lanes], dst_ref=z_full.at[:, lanes], send_sem=x_send, recv_sem=x_recv,
+    rings = ((0, 5), (5, 11), (11, plane))
+
+    def twin_copy(slot):
+        ring = [first <= slot < last for first, last in rings].index(True)
+        return pltpu.make_async_remote_copy(
+            src_ref=z_full.at[:, share_lanes(slot, 1)], dst_ref=z_full.at[:, share_lanes(plane + slot, 1)],
+            send_sem=x_send, recv_sem=x_recv.at[ring], device_id=twin, device_id_type=MESH)
+
+    def twin_arrival(ring):
+        first, last = rings[ring]
+        lanes = share_lanes(plane + first, last - first)
+        return pltpu.make_async_remote_copy(
+            src_ref=z_full.at[:, lanes], dst_ref=z_full.at[:, lanes], send_sem=x_send, recv_sem=x_recv.at[ring],
             device_id=twin, device_id_type=MESH)
 
     twin_all = pltpu.make_async_remote_copy(
-        src_ref=z_full.at[:, pl.ds(0, half_k)], dst_ref=z_full.at[:, pl.ds(0, half_k)],
-        send_sem=x_send, recv_sem=x_recv, device_id=twin, device_id_type=MESH)
+        src_ref=z_full.at[:, share_lanes(0, plane)], dst_ref=z_full.at[:, share_lanes(0, plane)],
+        send_sem=x_send, recv_sem=x_recv.at[0], device_id=twin, device_id_type=MESH)
     ghost_all = pltpu.make_async_remote_copy(
         src_ref=ghost_in, dst_ref=ghost_in, send_sem=g1_send, recv_sem=g1_recv, device_id=twin, device_id_type=MESH)
     feat_all = pltpu.make_async_remote_copy(
@@ -235,7 +247,6 @@
     pl.semaphore_wait(barrier, 4 + (members - 1) + (depth - 1))
     for block in (3, 2, 1, 0):
         ghost_copy(block).start()
-    spread_start(pos_all, p_send, p_recv)
 
     for fetch in fetches[3:]:
         fetch.wait()
@@ -296,16 +307,28 @@
     own_message = messages(0, pairs_own, own_feats)
 
     wv32[...] = jnp.zeros_like(wv32)
-    wv32[0:3, :] = wv_ref[...].astype(f32)
-    own_waves = wv32[:, chip_share((0, 0), core)]
-    share_waves[0:8, :] = own_waves
-    share_waves[8:16, :] = jnp.zeros_like(own_waves)
+    for slot in range(members):
+        dx, dy, _ = chip_offsets[slot % plane]
+        chip = lax.rem(my_x + dx, side) * side + lax.rem(my_y + dy, side)
+        owner = (core if slot < plane else 1 - core) * plane + chip
+        wv32[0:3, share_lanes(slot, 1)] = wv_ref[:, pl.ds(pl.multiple_of(owner * share, 128), share)].astype(f32)
+    own_waves = wv32[:, share_lanes(0, 1)]
     squared = jnp.sum(own_waves * own_waves, axis=0, keepdims=True)
     kweight = jnp.exp(-smearing * squared) / squared * scale
 
+    def atom_phases(step):
+        for part in range(8):
+            rows = pl.ds(pl.multiple_of(step * 2048 + part * 256, 256), 256)
+            cosines, sines = turns_cos_sin(dot_nn(wv32[:, rows].T.astype(bf16), own_coords), cos_fast, sin_fast)
+            atom_phase[rows, 0:atoms] = cosines.astype(bf16)
+            atom_phase[rows, atoms:2 * atoms] = sines.astype(bf16)
+
+    atom_steps = total_k // 2048
+    pl.loop(0, atom_steps // 2)(atom_phases)
+
     ghost_all.wait_recv()
-    lane_block = lax.broadcasted_iota(jnp.int32, (16, atoms), 1) // ghosts
-    ghost32 = jnp.zeros((16, atoms), f32)
+    lane_block = lax.broadcasted_iota(jnp.int32, (8, atoms), 1) // ghosts
+    ghost32 = jnp.zeros((8, atoms), f32)
     for block in range(4):
         ghost32 = jnp.where(lane_block == block, ghost_in[block].astype(f32), ghost32)
     ghost_cos, ghost_sin = turns_cos_sin(0.5 * ghost32, cos_fine, sin_fine)
@@ -317,86 +340,84 @@
     feat_out[...] = dot_nn(pick_rows, projected).astype(bf16)
     for block in (3, 2, 1, 0):
         feat_copy(block).start()
+    spread_start(pos_all, p_send, p_recv)
     own_message = messages(1, pairs_own, projected)
+    pl.loop(atom_steps // 2, atom_steps)(atom_phases)
+    ghost_all.wait_send()
+    feat_all.wait_recv()
+    hidden = update(1, hidden, own_message + messages(1, pairs_ghost, feat_in[...]))
+    charges = dot_nt(wch_ref[...], hidden)
+    q_all[:, 0:atoms] = charges.astype(bf16)
+    spread_start(q_all, q_send, q_recv)
+    feat_all.wait_send()
 
     spread_near(pos_all, p_send, p_recv)
     spread_far(pos_all, p_send, p_recv)
-    waves16 = share_waves[...].astype(bf16)
+    waves8 = own_waves.astype(bf16)
 
     def share_phases(step):
         for part in range(4):
             rows = pl.ds(pl.multiple_of(step * 512 + part * 128, 128), 128)
             places = pos_all[:, rows].astype(f32).T.astype(bf16)
-            cosines, sines = turns_cos_sin(dot_nn(places, waves16), cos_fast, sin_fast)
+            cosines, sines = turns_cos_sin(dot_nn(places, waves8), cos_fast, sin_fast)
             share_phase[rows, 0:share] = cosines.astype(bf16)
             share_phase[rows, share:2 * share] = sines.astype(bf16)
 
-    def atom_phases(step):
-        for part in range(8):
-            rows = pl.ds(pl.multiple_of(step * 2048 + part * 256, 256), 256)
-            waves = wv32[:, rows].T
-            waves = jnp.concatenate([waves, jnp.zeros_like(waves)], axis=1).astype(bf16)
-            cosines, sines = turns_cos_sin(dot_nn(waves, coords[...]), cos_fast, sin_fast)
-            atom_phase[rows, 0:atoms] = cosines.astype(bf16)
-            atom_phase[rows, atoms:2 * atoms] = sines.astype(bf16)
-
     share_steps = members * atoms // 512
-    atom_steps = total_k // 2048
     pl.loop(0, share_steps)(share_phases)
-    ghost_all.wait_send()
     spread_sent(pos_all, p_send, p_recv)
-
-    feat_all.wait_recv()
-    hidden = update(1, hidden, own_message + messages(1, pairs_ghost, feat_in[...]))
-    charges = dot_nt(wch_ref[...], hidden)
-    charges_high = charges.astype(bf16).astype(f32)
-    q_all[:, 0:atoms] = jnp.concatenate([charges_high, charges - charges_high], axis=0).astype(bf16)
-    spread_start(q_all, q_send, q_recv)
-    pl.loop(0, atom_steps // 2)(atom_phases)
-    feat_all.wait_send()
 
     near_lanes, far_lanes = slice(0, near_count * atoms), slice(near_count * atoms, members * atoms)
     spread_near(q_all, q_send, q_recv)
     both_parts = dot_nn(q_all[:, near_lanes], share_phase[near_lanes, :])
     spread_far(q_all, q_send, q_recv)
     both_parts = both_parts + dot_nn(q_all[:, far_lanes], share_phase[far_lanes, :])
-    both_parts = both_parts[:latent] + both_parts[latent:]
     z_out[...] = (jnp.concatenate([both_parts[:, :share], both_parts[:, share:]], axis=0) * kweight).astype(bf16)
     for dz in heights:
         column_copy(dz).start()
-    pl.loop(atom_steps // 2, atom_steps)(atom_phases)
     spread_sent(q_all, q_send, q_recv)
 
     column_all.wait_recv()
     summed = z_out[...].astype(f32)
     for dz in range(1, depth):
         summed = summed + z_in[dz - 1].astype(f32)
-    z_full[:, chip_share((0, 0), core)] = summed.astype(bf16)
+    z_full[:, share_lanes(0, 1)] = summed.astype(bf16)
     for number in range(plane - 1, 0, -1):
-        plane_copy(number, (0, 0)).start()
-    twin_copy((0, 0)).start()
+        plane_copy(number).start()
+    twin_copy(0).start()
     column_all.wait_send()
-    for number in range(1, plane):
-        source = opposite(chip_offsets[number])
-        plane_copy(number, source).wait_recv()
-        twin_copy(source).start()
+
+    def apply_slots(first, last):
+        for slot in range(first, last):
+            lanes = share_lanes(slot, 1)
+            block = z_full[:, lanes]
+            left[0:16, lanes] = block
+            block = block.astype(f32)
+            waves = wv32[:, lanes]
+            for d in range(3):
+                left[16 * (d + 1):16 * (d + 2), lanes] = (block * waves[d:d + 1, :]).astype(bf16)
+        lanes = share_lanes(first, last - first)
+        return dot_nn(left[:, lanes], atom_phase[lanes, :])
+
+    def take_ring(ring):
+        for slot in range(max(rings[ring][0], 1), rings[ring][1]):
+            plane_arrival(slot).wait_recv()
+            twin_copy(slot).start()
+
+    def take_twin_ring(ring):
+        twin_arrival(ring).wait_recv()
+        return apply_slots(plane + rings[ring][0], plane + rings[ring][1])
+
+    take_ring(0)
+    sums = apply_slots(*rings[0])
+    take_ring(1)
+    sums = sums + apply_slots(*rings[1])
+    take_ring(2)
+    sums = sums + take_twin_ring(0)
+    sums = sums + apply_slots(*rings[2])
+    sums = sums + take_twin_ring(1)
+    sums = sums + take_twin_ring(2)
     plane_all.wait_send()
-
-    def apply_half(which_core):
-        start = pl.multiple_of(which_core * half_k, half_k)
-        for first in range(0, half_k, 512):
-            lanes = pl.ds(pl.multiple_of(start + first, 512), 512)
-            block = z_full[:, lanes].astype(f32)
-            waves = wv32[:, lanes]
-            here = slice(first, first + 512)
-            left[0:16, here] = z_full[:, lanes]
-            for d in range(3):
-                left[16 * (d + 1):16 * (d + 2), here] = (block * waves[d:d + 1, :]).astype(bf16)
-        return dot_nn(left[...], atom_phase[pl.ds(start, half_k), :])
-
-    sums = apply_half(core)
-    twin_all.wait_recv()
-    sums = sums + apply_half(1 - core)
     by_cos, by_sin = sums[:, :atoms], sums[:, atoms:]
     out_ref[...] = jnp.zeros_like(out_ref)
     out_ref[0:latent, :] = by_cos[:latent] + by_sin[latent:2 * latent]
@@ -428,15 +449,13 @@
         in_specs=[hbm] * len(operands),
         out_specs=vmem,
         scratch_shapes=[pltpu.VMEM(value.shape, value.dtype) for value in operands] + [
-            pltpu.VMEM((16, atoms), f32),
-            pltpu.VMEM((16, atoms), bf16),
-            pltpu.VMEM((16, atoms), bf16),
-            pltpu.VMEM((4, 16, atoms), bf16),
             pltpu.VMEM((8, atoms), f32),
-            pltpu.VMEM((16, members * atoms), bf16),
-            pltpu.VMEM((16, members * atoms), bf16),
+            pltpu.VMEM((8, atoms), bf16),
+            pltpu.VMEM((4, 8, atoms), bf16),
+            pltpu.VMEM((8, atoms), f32),
+            pltpu.VMEM((8, members * atoms), bf16),
+            pltpu.VMEM((latent, members * atoms), bf16),
             pltpu.VMEM((8, total_k), f32),
-            pltpu.VMEM((16, share), f32),
             pltpu.VMEM((members * atoms, 2 * share), bf16),
             pltpu.VMEM((total_k, 2 * atoms), bf16),
             pltpu.VMEM((bases * atoms, 2 * atoms), bf16),
@@ -446,9 +465,9 @@
             pltpu.VMEM((16, share), bf16),
             pltpu.VMEM((depth - 1, 16, share), bf16),
             pltpu.VMEM((16, total_k), bf16),
-            pltpu.VMEM((64, total_k // 2), bf16),
+            pltpu.VMEM((64, total_k), bf16),
             dma((len(operands),)), dma, dma, dma, dma, dma, dma((2,)), dma, dma((2,)),
-            dma, dma, dma, dma((plane,)), dma, dma,
+            dma, dma, dma, dma((plane,)), dma, dma((3,)),
         ],
         compiler_params=pltpu.CompilerParams(
             collective_id=0, has_side_effects=True, vmem_limit_bytes=60 * 1024 * 1024

time: 47.2 us -> 48.5 us (1.028)
  Pallas kernels: 43.8 us -> 45.1 us
    pallas_call x1, Pallas kernels: 43.8 us -> 45.1 us  [per_device(): pl.pallas_call(functools.partial(kernel, scale), out_shape=jax.ShapeDtype...]
where the time goes in v3:
time: 48.5 us; the launch traced here: 48.3 us
  Pallas kernels  45.1 us (93%)
  local copies, waits for them, and re-layouts  2.53 us (5%)
  between operations  0.64 us (1%)
    pallas_call x1, Pallas kernels, per_device(): pl.pallas_call(functools.partial(kernel, scale), out_shape=jax.ShapeDtype...  45.1 us
    slice x2, local copies, waits for them, and re-layouts, per_device(): return (packed[:latent], packed[latent:latent + 3])  2.53 us

profile of v3, /device:TPU:1, one launch (start us, length us, event | category | flops | bytes accessed | tf_op | source)
XLA Modules:
  0.0 48.3 jit_solution(16487162696426832867)
XLA Ops:
  0.6 45.1 %ewald_step.1 = f32[16,128]{1,0:T(8,128)} custom-call(bf16[3,128]{1,0:T(4,128)(2,1)} %pos_hbm.1, s32[1,128]{1,0:T(1,128)} %bitcast.3, s32[4,32]{1,0:T(4,128)} %gr_hbm.1, s32[64,128]{1,0:T(8,128)} %nbr_hbm.1, s32[3,12288]{1,0:T(4,128)} %wv_hbm.1, bf16[2,128]{1,0:T(2,128)(2,1)} %emb_hbm.1, bf16[2,128,128]{2,1,0:T(8,128)(2,1)} %win_hbm.1, ...), custom_call_target="tpu_custom_call" | custom-call | tf_op jit(solution)/shard_map/ewald_step/pallas_call | solution.py:446
  45.8 1.3 %slice.7 = f32[3,128]{1,0:T(4,128)} slice(f32[16,128]{1,0:T(8,128)} %ewald_step.1), slice={[8:11], [0:128]} | slice | bytes 3072 | tf_op jit(solution)/shard_map/slice | solution.py:477
  47.0 1.3 %slice.6 = f32[8,128]{1,0:T(8,128)} slice(f32[16,128]{1,0:T(8,128)} %ewald_step.1), slice={[0:8], [0:128]} | slice | bytes 8192 | tf_op jit(solution)/shard_map/slice | solution.py:477

commit v4 on v3

--- a/solution.py
+++ b/solution.py
@@ -35,6 +35,10 @@
     return fit_series(lambda t: np.sin(2.0 * np.pi * t) / t, terms)
 
 
+half_sin = fit_series(lambda t: math.sqrt(2.0) * np.sin(np.pi * t) / t, 4)
+half_cos = fit_series(lambda t: math.sqrt(2.0) * np.cos(np.pi * t), 4)
+
+
 def horner(coefs, u):
     value = coefs[-1]
     for c in coefs[-2::-1]:
@@ -48,6 +52,13 @@
     return horner(cos_coefs, u), t * horner(sin_coefs, u)
 
 
+def phase_pair(turns):
+    t = turns - ((turns + round_magic) - round_magic)
+    u = t * t
+    s = t * horner(half_sin, u)
+    return 1.0 - s * s, s * horner(half_cos, u)
+
+
 def dot_nt(a, b):
     return lax.dot_general(a, b, (((1,), (1,)), ((), ())), preferred_element_type=f32)
 
@@ -70,9 +81,9 @@
     pos_hbm, spec_hbm, gr_hbm, nbr_hbm, wv_hbm, emb_hbm, win_hbm, rad_hbm, gain_hbm, wout_hbm, wch_hbm,
     out_ref,
     pos_ref, spec_ref, gr_ref, nbr_ref, wv_ref, emb_ref, win_ref, rad_ref, gain_ref, wout_ref, wch_ref,
-    c32, ghost_out, ghost_in, gpad, pos_all, q_all, wv32,
-    share_phase, atom_phase, pairs_own, pairs_ghost, feat_out, feat_in, z_out, z_in, z_full, left,
-    in_sem, g1_send, g1_recv, g2_send, g2_recv, p_send, p_recv, q_send, q_recv,
+    c32, tiles, near_coords, gpad, pos_all, q_all, wv32,
+    share_phase, atom_phase, pairs_own, pairs_ghost, pairs_kind, count_out, count_in, z_out, z_in, z_full, left,
+    in_sem, g1_send, g1_recv, g2_send, g2_recv, g3_send, g3_recv, p_send, p_recv, q_send, q_recv,
     zs_send, zs_recv, w_send, w_recv, x_send, x_recv,
 ):
     dom = lax.axis_index("dom")
@@ -99,12 +110,21 @@
         index = lax.rem(z_me + dz, depth)
         return (lax.rem(index, depth // 2) * plane + xy, (index // (depth // 2)) * 2 + core)
 
-    neighbours_at = (
-        (lax.rem(dom + 1, n_dom), sub),
-        (lax.rem(dom + n_dom - 1, n_dom), sub),
-        (dom, lax.rem(sub + 1, n_sub)),
-        (dom, lax.rem(sub + n_sub - 1, n_sub)),
-    )
+    steps = ((-1, 0), (1, 0), (0, -1), (0, 1))
+    around = ((0, -1), (0, 1), (-1, -1), (-1, 1), (1, -1), (1, 1), (0, 2), (-1, 0), (1, 0), (-2, 0), (2, 0))
+
+    def place(step):
+        return (step[0], step[1] % 4)
+
+    def beside(step):
+        return (lax.rem(dom + step[0] + n_dom, n_dom), lax.rem(sub + step[1] + n_sub, n_sub))
+
+    def reverse(step):
+        return (-step[0], -step[1])
+
+    tile_of = {place(step): number for number, step in enumerate(around)}
+    tile_of[(0, 0)] = len(around)
+    neighbours_at = tuple(beside(reverse(step)) for step in steps)
     offsets = torus_offsets()
     slot_of = {offset: slot for slot, offset in enumerate(offsets)}
     chip_offsets = [offset for offset in offsets if offset[2] == 0]
@@ -122,8 +142,8 @@
     def greet(target):
         pl.semaphore_signal(barrier, inc=1, device_id=target, device_id_type=MESH)
 
-    for target in neighbours_at[::-1]:
-        greet(target)
+    for step in around:
+        greet(beside(step))
     for fetch in fetches[:3]:
         fetch.start()
     for offset in offsets[:0:-1]:
@@ -148,18 +168,24 @@
         picks = picks + pltpu.roll(grown, block * ghosts, axis=1)[source:source + 1, :]
     row_number = lax.broadcasted_iota(jnp.int32, (atoms, atoms), 0).astype(f32)
     pick_cols = jnp.where(row_number == picks, 1.0, 0.0)
-    ghost_out[...] = dot_nn(own_coords, pick_cols.astype(bf16)).astype(bf16)
+    pick_cols = pick_cols.astype(bf16)
+    tiles[len(around)] = dot_nn(own_coords, pick_cols).astype(bf16)
     pos_all[:, 0:atoms] = own_coords
 
-    def ghost_copy(block):
-        return pltpu.make_async_remote_copy(
-            src_ref=ghost_out, dst_ref=ghost_in.at[block], send_sem=g1_send, recv_sem=g1_recv,
+    def tile_copy(step):
+        return pltpu.make_async_remote_copy(
+            src_ref=tiles.at[len(around)], dst_ref=tiles.at[tile_of[place(reverse(step))]], send_sem=g1_send,
+            recv_sem=g1_recv, device_id=beside(step), device_id_type=MESH)
+
+    def near_copy(block):
+        return pltpu.make_async_remote_copy(
+            src_ref=pos_all.at[:, pl.ds(0, atoms)], dst_ref=near_coords.at[block], send_sem=g2_send, recv_sem=g2_recv,
             device_id=neighbours_at[block], device_id_type=MESH)
 
-    def feat_copy(block):
+    def count_copy(block):
         rows = pl.ds(block * ghosts, ghosts)
         return pltpu.make_async_remote_copy(
-            src_ref=feat_out.at[rows], dst_ref=feat_in.at[rows], send_sem=g2_send, recv_sem=g2_recv,
+            src_ref=count_out.at[rows], dst_ref=count_in.at[rows], send_sem=g3_send, recv_sem=g3_recv,
             device_id=neighbours_at[block], device_id_type=MESH)
 
     def slot_lanes(first, count):
@@ -239,14 +265,19 @@
     twin_all = pltpu.make_async_remote_copy(
         src_ref=z_full.at[:, share_lanes(0, plane)], dst_ref=z_full.at[:, share_lanes(0, plane)],
         send_sem=x_send, recv_sem=x_recv.at[0], device_id=twin, device_id_type=MESH)
-    ghost_all = pltpu.make_async_remote_copy(
-        src_ref=ghost_in, dst_ref=ghost_in, send_sem=g1_send, recv_sem=g1_recv, device_id=twin, device_id_type=MESH)
-    feat_all = pltpu.make_async_remote_copy(
-        src_ref=feat_in, dst_ref=feat_in, send_sem=g2_send, recv_sem=g2_recv, device_id=twin, device_id_type=MESH)
-
-    pl.semaphore_wait(barrier, 4 + (members - 1) + (depth - 1))
+    tiles_all = pltpu.make_async_remote_copy(
+        src_ref=tiles.at[pl.ds(0, len(around))], dst_ref=tiles.at[pl.ds(0, len(around))], send_sem=g1_send,
+        recv_sem=g1_recv, device_id=twin, device_id_type=MESH)
+    near_all = pltpu.make_async_remote_copy(
+        src_ref=near_coords, dst_ref=near_coords, send_sem=g2_send, recv_sem=g2_recv, device_id=twin, device_id_type=MESH)
+    count_all = pltpu.make_async_remote_copy(
+        src_ref=count_in, dst_ref=count_in, send_sem=g3_send, recv_sem=g3_recv, device_id=twin, device_id_type=MESH)
+
+    pl.semaphore_wait(barrier, len(around) + (members - 1) + (depth - 1))
+    for step in around:
+        tile_copy(step).start()
     for block in (3, 2, 1, 0):
-        ghost_copy(block).start()
+        near_copy(block).start()
 
     for fetch in fetches[3:]:
         fetch.wait()
@@ -258,12 +289,15 @@
         for slot in range(listed.shape[0]):
             counted = jnp.where(table_row == listed[slot:slot + 1, :], counted + 1.0, counted)
         quarters.append(counted)
-    own_counts = jnp.concatenate(quarters[:2], axis=0).T
-    ghost_counts = jnp.concatenate(quarters[2:], axis=0).T
-    pick_rows = pick_cols.T.astype(bf16)
+    own_counts_t, ghost_counts_t = jnp.concatenate(quarters[:2], axis=0), jnp.concatenate(quarters[2:], axis=0)
+    count_out[:, 0:atoms] = dot_nn(own_counts_t.astype(bf16), pick_cols).T.astype(bf16)
+    count_out[:, atoms:2 * atoms] = dot_nn(ghost_counts_t.astype(bf16), pick_cols).T.astype(bf16)
+    for block in (3, 2, 1, 0):
+        count_copy(block).start()
+    spread_start(pos_all, p_send, p_recv)
+    own_counts, ghost_counts = own_counts_t.T, ghost_counts_t.T
 
     cos_fine, sin_fine = cos_series(9), sin_series(9)
-    cos_fast, sin_fast = cos_series(6), sin_series(5)
     own_cos, own_sin = turns_cos_sin(0.5 * own32, cos_fine, sin_fine)
     own_cos_col, own_sin_col = own_cos.T, own_sin.T
     embedding = emb_ref[...].astype(f32)
@@ -290,7 +324,9 @@
             basis = basis * basis
 
     def messages(number, pairs, feats):
-        products = dot_nn(pairs[...], jnp.concatenate([feats, feats], axis=0))
+        return radial_sum(number, dot_nn(pairs[...], jnp.concatenate([feats, feats], axis=0)))
+
+    def radial_sum(number, products):
         radial_layer = rad_ref[number].astype(f32)
         message = radial_layer[0:1, :] * products[:atoms]
         for b in range(1, bases):
@@ -313,58 +349,95 @@
         owner = (core if slot < plane else 1 - core) * plane + chip
         wv32[0:3, share_lanes(slot, 1)] = wv_ref[:, pl.ds(pl.multiple_of(owner * share, 128), share)].astype(f32)
     own_waves = wv32[:, share_lanes(0, 1)]
-    squared = jnp.sum(own_waves * own_waves, axis=0, keepdims=True)
-    kweight = jnp.exp(-smearing * squared) / squared * scale
+    waves8 = own_waves.astype(bf16)
+
+    def share_phases(step):
+        for part in range(8):
+            rows = pl.ds(pl.multiple_of(step * 1024 + part * 128, 128), 128)
+            places = pos_all[:, rows].astype(f32).T.astype(bf16)
+            cosines, sines = phase_pair(dot_nn(places, waves8))
+            share_phase[rows, 0:share] = cosines.astype(bf16)
+            share_phase[rows, share:2 * share] = sines.astype(bf16)
 
     def atom_phases(step):
         for part in range(8):
             rows = pl.ds(pl.multiple_of(step * 2048 + part * 256, 256), 256)
-            cosines, sines = turns_cos_sin(dot_nn(wv32[:, rows].T.astype(bf16), own_coords), cos_fast, sin_fast)
+            cosines, sines = phase_pair(dot_nn(wv32[:, rows].T.astype(bf16), own_coords))
             atom_phase[rows, 0:atoms] = cosines.astype(bf16)
             atom_phase[rows, atoms:2 * atoms] = sines.astype(bf16)
 
-    atom_steps = total_k // 2048
-    pl.loop(0, atom_steps // 2)(atom_phases)
-
-    ghost_all.wait_recv()
+    squared = jnp.sum(own_waves * own_waves, axis=0, keepdims=True)
+    kweight = jnp.exp(-smearing * squared) / squared * scale
+
+    pl.loop(0, 2)(atom_phases)
+    tiles_all.wait_recv()
+    near_all.wait_recv()
     lane_block = lax.broadcasted_iota(jnp.int32, (8, atoms), 1) // ghosts
-    ghost32 = jnp.zeros((8, atoms), f32)
-    for block in range(4):
-        ghost32 = jnp.where(lane_block == block, ghost_in[block].astype(f32), ghost32)
-    ghost_cos, ghost_sin = turns_cos_sin(0.5 * ghost32, cos_fine, sin_fine)
+
+    def ghosts_of(step):
+        merged = jnp.zeros((8, atoms), f32)
+        for block in range(4):
+            source = place((step[0] + steps[block][0], step[1] + steps[block][1]))
+            merged = jnp.where(lane_block == block, tiles[tile_of[source]].astype(f32), merged)
+        return merged
+
+    ghost32 = ghosts_of((0, 0))
+    tables = [ghost32] + [near_coords[block].astype(f32) for block in range(4)] + [ghosts_of(step) for step in steps]
+    table_cos, table_sin = turns_cos_sin(0.5 * jnp.concatenate(tables, axis=0), cos_fine, sin_fine)
+    ghost_cos, ghost_sin = table_cos[0:8], table_sin[0:8]
     fill_pairs(pairs_ghost, ghost_counts, ghost_cos, ghost_sin)
     ghost_second = ghost32.T[:, 3:4] > 0.5
     ghost_feats = jnp.where(ghost_second, projected_kinds[1:2, :], projected_kinds[0:1, :]).astype(bf16)
-    hidden = update(0, hidden, own_message + messages(0, pairs_ghost, ghost_feats))
-    projected = dot_nn(hidden, win_ref[1]).astype(bf16)
-    feat_out[...] = dot_nn(pick_rows, projected).astype(bf16)
-    for block in (3, 2, 1, 0):
-        feat_copy(block).start()
-    spread_start(pos_all, p_send, p_recv)
-    own_message = messages(1, pairs_own, projected)
-    pl.loop(atom_steps // 2, atom_steps)(atom_phases)
-    ghost_all.wait_send()
-    feat_all.wait_recv()
-    hidden = update(1, hidden, own_message + messages(1, pairs_ghost, feat_in[...]))
+
+    ghost_cos_col, ghost_sin_col = ghost_cos.T, ghost_sin.T
+    count_all.wait_recv()
+    halves = []
+    for half in range(2):
+        chords, kinds = [], []
+        for block in range(4):
+            entry = 1 + half * 4 + block
+            rows = slice(block * ghosts, (block + 1) * ghosts)
+            chord = jnp.zeros((ghosts, atoms), f32)
+            for d in range(3):
+                at = entry * 8 + d
+                apart = table_sin[at:at + 1, :] * ghost_cos_col[rows, d:d + 1] - table_cos[at:at + 1, :] * ghost_sin_col[rows, d:d + 1]
+                chord = chord + apart * apart
+            chords.append(chord)
+            kinds.append(jnp.broadcast_to(tables[entry][3:4, :], (ghosts, atoms)))
+        basis = jnp.exp(-0.125 * jnp.concatenate(chords, axis=0))
+        halves.append([basis, count_in[:, half * atoms:(half + 1) * atoms].astype(f32), jnp.concatenate(kinds, axis=0)])
+    for b in range(bases):
+        pair0, pair1 = (basis * counts for basis, counts, _ in halves)
+        second = pair0 * halves[0][2] + pair1 * halves[1][2]
+        first = pair0 + pair1 - second
+        rows = slice(b * atoms, (b + 1) * atoms)
+        for number, part in enumerate((first, second)):
+            high = part.astype(bf16)
+            pairs_kind[rows, 2 * number * atoms:(2 * number + 1) * atoms] = high
+            pairs_kind[rows, (2 * number + 1) * atoms:(2 * number + 2) * atoms] = (part - high.astype(f32)).astype(bf16)
+        for half in halves:
+            half[0] = half[0] * half[0]
+    kind_rows = jnp.concatenate(
+        [jnp.broadcast_to(projected_kinds[kind:kind + 1, :], (2 * atoms, projected_kinds.shape[1])) for kind in range(2)],
+        axis=0).astype(bf16)
+    ghost_message = radial_sum(0, dot_nn(pairs_kind[...], kind_rows))
+    message = jnp.concatenate([own_message + messages(0, pairs_ghost, ghost_feats), ghost_message], axis=0)
+    ghost_hidden = jnp.where(ghost_second, embedding[1:2, :], embedding[0:1, :])
+    everyone = update(0, jnp.concatenate([hidden, ghost_hidden], axis=0), message)
+    hidden = everyone[:atoms]
+    projected = dot_nn(everyone, win_ref[1]).astype(bf16)
+    message = messages(1, pairs_own, projected[:atoms]) + messages(1, pairs_ghost, projected[atoms:])
+    hidden = update(1, hidden, message)
     charges = dot_nt(wch_ref[...], hidden)
     q_all[:, 0:atoms] = charges.astype(bf16)
     spread_start(q_all, q_send, q_recv)
-    feat_all.wait_send()
+    tiles_all.wait_send()
+    near_all.wait_send()
+    count_all.wait_send()
 
     spread_near(pos_all, p_send, p_recv)
     spread_far(pos_all, p_send, p_recv)
-    waves8 = own_waves.astype(bf16)
-
-    def share_phases(step):
-        for part in range(4):
-            rows = pl.ds(pl.multiple_of(step * 512 + part * 128, 128), 128)
-            places = pos_all[:, rows].astype(f32).T.astype(bf16)
-            cosines, sines = turns_cos_sin(dot_nn(places, waves8), cos_fast, sin_fast)
-            share_phase[rows, 0:share] = cosines.astype(bf16)
-            share_phase[rows, share:2 * share] = sines.astype(bf16)
-
-    share_steps = members * atoms // 512
-    pl.loop(0, share_steps)(share_phases)
+    pl.loop(0, 4)(share_phases)
     spread_sent(pos_all, p_send, p_recv)
 
     near_lanes, far_lanes = slice(0, near_count * atoms), slice(near_count * atoms, members * atoms)
@@ -375,6 +448,7 @@
     z_out[...] = (jnp.concatenate([both_parts[:, :share], both_parts[:, share:]], axis=0) * kweight).astype(bf16)
     for dz in heights:
         column_copy(dz).start()
+    pl.loop(2, 6)(atom_phases)
     spread_sent(q_all, q_send, q_recv)
 
     column_all.wait_recv()
@@ -432,7 +506,6 @@
     atoms = positions.shape[1]
     total_k = wavevectors.shape[1]
     latent = w_charge.shape[1]
-    channels = w_in.shape[2]
     bases = radial.shape[1]
     share = total_k // members
     scale = 1.0 / math.sqrt(atoms * lax.axis_size(("dom", "sub")))
@@ -450,7 +523,7 @@
         out_specs=vmem,
         scratch_shapes=[pltpu.VMEM(value.shape, value.dtype) for value in operands] + [
             pltpu.VMEM((8, atoms), f32),
-            pltpu.VMEM((8, atoms), bf16),
+            pltpu.VMEM((12, 8, atoms), bf16),
             pltpu.VMEM((4, 8, atoms), bf16),
             pltpu.VMEM((8, atoms), f32),
             pltpu.VMEM((8, members * atoms), bf16),
@@ -460,13 +533,14 @@
             pltpu.VMEM((total_k, 2 * atoms), bf16),
             pltpu.VMEM((bases * atoms, 2 * atoms), bf16),
             pltpu.VMEM((bases * atoms, 2 * atoms), bf16),
-            pltpu.VMEM((atoms, channels), bf16),
-            pltpu.VMEM((atoms, channels), bf16),
+            pltpu.VMEM((bases * atoms, 4 * atoms), bf16),
+            pltpu.VMEM((atoms, 2 * atoms), bf16),
+            pltpu.VMEM((atoms, 2 * atoms), bf16),
             pltpu.VMEM((16, share), bf16),
             pltpu.VMEM((depth - 1, 16, share), bf16),
             pltpu.VMEM((16, total_k), bf16),
             pltpu.VMEM((64, total_k), bf16),
-            dma((len(operands),)), dma, dma, dma, dma, dma, dma((2,)), dma, dma((2,)),
+            dma((len(operands),)), dma, dma, dma, dma, dma, dma, dma, dma((2,)), dma, dma((2,)),
             dma, dma, dma, dma((plane,)), dma, dma((3,)),
         ],
         compiler_params=pltpu.CompilerParams(

time: 48.5 us -> 44.1 us (0.909)
  Pallas kernels: 45.1 us -> 40.8 us
    pallas_call x1, Pallas kernels: 45.1 us -> 40.8 us  [per_device(): pl.pallas_call(functools.partial(kernel, scale), out_shape=jax.ShapeDtype...]
where the time goes in v4:
time: 44.1 us; the launch traced here: 44 us
  Pallas kernels  40.8 us (93%)
  local copies, waits for them, and re-layouts  2.53 us (6%)
  between operations  0.64 us (1%)
    pallas_call x1, Pallas kernels, per_device(): pl.pallas_call(functools.partial(kernel, scale), out_shape=jax.ShapeDtype...  40.8 us
    slice x2, local copies, waits for them, and re-layouts, per_device(): return (packed[:latent], packed[latent:latent + 3])  2.53 us

profile of v4, /device:TPU:1, one launch (start us, length us, event | category | flops | bytes accessed | tf_op | source)
XLA Modules:
  0.0 44.0 jit_solution(6547154662471428876)
XLA Ops:
  0.6 40.8 %ewald_step.1 = f32[16,128]{1,0:T(8,128)} custom-call(bf16[3,128]{1,0:T(4,128)(2,1)} %pos_hbm.1, s32[1,128]{1,0:T(1,128)} %bitcast.3, s32[4,32]{1,0:T(4,128)} %gr_hbm.1, s32[64,128]{1,0:T(8,128)} %nbr_hbm.1, s32[3,12288]{1,0:T(4,128)} %wv_hbm.1, bf16[2,128]{1,0:T(2,128)(2,1)} %emb_hbm.1, bf16[2,128,128]{2,1,0:T(8,128)(2,1)} %win_hbm.1, ...), custom_call_target="tpu_custom_call" | custom-call | tf_op jit(solution)/shard_map/ewald_step/pallas_call | solution.py:519
  41.4 1.3 %slice.7 = f32[3,128]{1,0:T(4,128)} slice(f32[16,128]{1,0:T(8,128)} %ewald_step.1), slice={[8:11], [0:128]} | slice | bytes 3072 | tf_op jit(solution)/shard_map/slice | solution.py:551
  42.7 1.3 %slice.6 = f32[8,128]{1,0:T(8,128)} slice(f32[16,128]{1,0:T(8,128)} %ewald_step.1), slice={[0:8], [0:128]} | slice | bytes 8192 | tf_op jit(solution)/shard_map/slice | solution.py:551

commit v5 on v4

--- a/solution.py
+++ b/solution.py
@@ -79,7 +79,7 @@
 def kernel(
     scale,
     pos_hbm, spec_hbm, gr_hbm, nbr_hbm, wv_hbm, emb_hbm, win_hbm, rad_hbm, gain_hbm, wout_hbm, wch_hbm,
-    out_ref,
+    pot_ref, force_ref,
     pos_ref, spec_ref, gr_ref, nbr_ref, wv_ref, emb_ref, win_ref, rad_ref, gain_ref, wout_ref, wch_ref,
     c32, tiles, near_coords, gpad, pos_all, q_all, wv32,
     share_phase, atom_phase, pairs_own, pairs_ghost, pairs_kind, count_out, count_in, z_out, z_in, z_full, left,
@@ -483,22 +483,21 @@
         return apply_slots(plane + rings[ring][0], plane + rings[ring][1])
 
     take_ring(0)
+    take_ring(1)
     sums = apply_slots(*rings[0])
-    take_ring(1)
+    take_ring(2)
     sums = sums + apply_slots(*rings[1])
-    take_ring(2)
     sums = sums + take_twin_ring(0)
     sums = sums + apply_slots(*rings[2])
     sums = sums + take_twin_ring(1)
     sums = sums + take_twin_ring(2)
     plane_all.wait_send()
     by_cos, by_sin = sums[:, :atoms], sums[:, atoms:]
-    out_ref[...] = jnp.zeros_like(out_ref)
-    out_ref[0:latent, :] = by_cos[:latent] + by_sin[latent:2 * latent]
+    pot_ref[...] = by_cos[:latent] + by_sin[latent:2 * latent]
     for d in range(3):
         first = 2 * latent * (d + 1)
         inner = by_sin[first:first + latent] - by_cos[first + latent:first + 2 * latent]
-        out_ref[latent + d:latent + d + 1, :] = jnp.sum(charges * inner, axis=0, keepdims=True)
+        force_ref[d:d + 1, :] = jnp.sum(charges * inner, axis=0, keepdims=True)
     twin_all.wait_send()
 
 
@@ -516,11 +515,11 @@
     dma = pltpu.SemaphoreType.DMA
     vmem = pl.BlockSpec(memory_space=pltpu.VMEM)
     hbm = pl.BlockSpec(memory_space=pltpu.HBM)
-    packed = pl.pallas_call(
+    return pl.pallas_call(
         functools.partial(kernel, scale),
-        out_shape=jax.ShapeDtypeStruct((16, atoms), f32),
+        out_shape=(jax.ShapeDtypeStruct((latent, atoms), f32), jax.ShapeDtypeStruct((3, atoms), f32)),
         in_specs=[hbm] * len(operands),
-        out_specs=vmem,
+        out_specs=(vmem, vmem),
         scratch_shapes=[pltpu.VMEM(value.shape, value.dtype) for value in operands] + [
             pltpu.VMEM((8, atoms), f32),
             pltpu.VMEM((12, 8, atoms), bf16),
@@ -544,11 +543,10 @@
             dma, dma, dma, dma((plane,)), dma, dma((3,)),
         ],
         compiler_params=pltpu.CompilerParams(
-            collective_id=0, has_side_effects=True, vmem_limit_bytes=60 * 1024 * 1024
+            collective_id=0, has_side_effects=True, vmem_limit_bytes=48 * 1024 * 1024
         ),
         name="ewald_step",
-    )(*operands)
-    return packed[:latent], packed[latent:latent + 3]
+    )(*[pltpu.with_memory_space_constraint(value, pltpu.HBM) for value in operands])
 
 
 def solution(mesh):

time: 44.1 us -> 41.7 us (0.946)
  local copies, waits for them, and re-layouts: 2.53 us -> 1.17 us
  Pallas kernels: 40.8 us -> 39.7 us
    slice x2 -> x0, local copies, waits for them, and re-layouts: 2.53 us -> none  [per_device(): return (packed[:latent], packed[latent:latent + 3])]
    unnamed x0 -> x2, local copies, waits for them, and re-layouts: none -> 1.17 us
    pallas_call x1, Pallas kernels: 40.8 us -> 39.7 us  [per_device(): pl.pallas_call(functools.partial(kernel, scale), out_shape=(jax.ShapeDtyp...]
where the time goes in v5:
time: 41.7 us; the launch traced here: 41.6 us
  Pallas kernels  39.7 us (95%)
  local copies, waits for them, and re-layouts  1.17 us (3%)
  between operations  0.64 us (2%)
    pallas_call x1, Pallas kernels, per_device(): pl.pallas_call(functools.partial(kernel, scale), out_shape=(jax.ShapeDtyp...  39.7 us
    unnamed x2, local copies, waits for them, and re-layouts  1.17 us

profile of v5, /device:TPU:1, one launch (start us, length us, event | category | flops | bytes accessed | tf_op | source)
XLA Modules:
  0.0 41.6 jit_solution(1104459338676935393)
XLA Ops:
  0.6 39.7 %ewald_step.1 = (f32[8,128]{1,0:T(8,128)S(1)}, f32[3,128]{1,0:T(4,128)S(1)}) custom-call(bf16[3,128]{1,0:T(4,128)(2,1)} %pos_hbm.1, s32[1,128]{1,0:T(1,128)} %bitcast.3, s32[4,32]{1,0:T(4,128)} %gr_hbm.1, s32[64,128]{1,0:T(8,128)} %nbr_hbm.1, s32[3,12288]{1,0:T(4,128)} %wv_hbm.1, bf16[2,128]{1,0:T(2,128)(2,1)} %emb_hbm.1, bf16[2,128,128]{2,1,0:T(8,128)(2,1)} %win_hbm.1, ...), custom_call_target="tpu_custom_call" | custom-call | tf_op jit(solution)/shard_map/ewald_step/pallas_call | solution.py:518
  40.4 0.6 %copy.15 = f32[8,128]{1,0:T(8,128)} copy(f32[8,128]{1,0:T(8,128)S(1)} %get-tuple-element.4) | data formatting | bytes 8192
  41.0 0.6 %copy.16 = f32[3,128]{1,0:T(4,128)} copy(f32[3,128]{1,0:T(4,128)S(1)} %get-tuple-element.5) | data formatting | bytes 3072

commit v6 on v5

--- a/solution.py
+++ b/solution.py
@@ -352,8 +352,8 @@
     waves8 = own_waves.astype(bf16)
 
     def share_phases(step):
-        for part in range(8):
-            rows = pl.ds(pl.multiple_of(step * 1024 + part * 128, 128), 128)
+        for part in range(16):
+            rows = pl.ds(pl.multiple_of(step * 2048 + part * 128, 128), 128)
             places = pos_all[:, rows].astype(f32).T.astype(bf16)
             cosines, sines = phase_pair(dot_nn(places, waves8))
             share_phase[rows, 0:share] = cosines.astype(bf16)
@@ -437,7 +437,7 @@
 
     spread_near(pos_all, p_send, p_recv)
     spread_far(pos_all, p_send, p_recv)
-    pl.loop(0, 4)(share_phases)
+    pl.loop(0, 2)(share_phases)
     spread_sent(pos_all, p_send, p_recv)
 
     near_lanes, far_lanes = slice(0, near_count * atoms), slice(near_count * atoms, members * atoms)

time: 41.7 us -> 41.3 us (level)
  no operation moved by 1% of the time
where the time goes in v6:
time: 41.3 us; the launch traced here: 41.2 us
  Pallas kernels  39.4 us (95%)
  local copies, waits for them, and re-layouts  1.17 us (3%)
  between operations  0.64 us (2%)
    pallas_call x1, Pallas kernels, per_device(): pl.pallas_call(functools.partial(kernel, scale), out_shape=(jax.ShapeDtyp...  39.4 us
    unnamed x2, local copies, waits for them, and re-layouts  1.17 us

profile of v6, /device:TPU:1, one launch (start us, length us, event | category | flops | bytes accessed | tf_op | source)
XLA Modules:
  0.0 41.2 jit_solution(6943589269055873051)
XLA Ops:
  0.6 39.4 %ewald_step.1 = (f32[8,128]{1,0:T(8,128)S(1)}, f32[3,128]{1,0:T(4,128)S(1)}) custom-call(bf16[3,128]{1,0:T(4,128)(2,1)} %pos_hbm.1, s32[1,128]{1,0:T(1,128)} %bitcast.3, s32[4,32]{1,0:T(4,128)} %gr_hbm.1, s32[64,128]{1,0:T(8,128)} %nbr_hbm.1, s32[3,12288]{1,0:T(4,128)} %wv_hbm.1, bf16[2,128]{1,0:T(2,128)(2,1)} %emb_hbm.1, bf16[2,128,128]{2,1,0:T(8,128)(2,1)} %win_hbm.1, ...), custom_call_target="tpu_custom_call" | custom-call | tf_op jit(solution)/shard_map/ewald_step/pallas_call | solution.py:518
  40.0 0.6 %copy.15 = f32[8,128]{1,0:T(8,128)} copy(f32[8,128]{1,0:T(8,128)S(1)} %get-tuple-element.4) | data formatting | bytes 8192
  40.6 0.6 %copy.16 = f32[3,128]{1,0:T(4,128)} copy(f32[3,128]{1,0:T(4,128)S(1)} %get-tuple-element.5) | data formatting | bytes 3072

commit v7 on v6

--- a/solution.py
+++ b/solution.py
@@ -484,9 +484,8 @@
 
     take_ring(0)
     take_ring(1)
-    sums = apply_slots(*rings[0])
     take_ring(2)
-    sums = sums + apply_slots(*rings[1])
+    sums = apply_slots(0, rings[1][1])
     sums = sums + take_twin_ring(0)
     sums = sums + apply_slots(*rings[2])
     sums = sums + take_twin_ring(1)

time: 41.3 us -> 41.3 us (level)
  no operation moved by 1% of the time
where the time goes in v7:
time: 41.3 us; the launch traced here: 41.2 us
  Pallas kernels  39.4 us (95%)
  local copies, waits for them, and re-layouts  1.17 us (3%)
  between operations  0.64 us (2%)
    pallas_call x1, Pallas kernels, per_device(): pl.pallas_call(functools.partial(kernel, scale), out_shape=(jax.ShapeDtyp...  39.4 us
    unnamed x2, local copies, waits for them, and re-layouts  1.17 us

profile of v7, /device:TPU:1, one launch (start us, length us, event | category | flops | bytes accessed | tf_op | source)
XLA Modules:
  0.0 41.2 jit_solution(473976911978907878)
XLA Ops:
  0.6 39.4 %ewald_step.1 = (f32[8,128]{1,0:T(8,128)S(1)}, f32[3,128]{1,0:T(4,128)S(1)}) custom-call(bf16[3,128]{1,0:T(4,128)(2,1)} %pos_hbm.1, s32[1,128]{1,0:T(1,128)} %bitcast.3, s32[4,32]{1,0:T(4,128)} %gr_hbm.1, s32[64,128]{1,0:T(8,128)} %nbr_hbm.1, s32[3,12288]{1,0:T(4,128)} %wv_hbm.1, bf16[2,128]{1,0:T(2,128)(2,1)} %emb_hbm.1, bf16[2,128,128]{2,1,0:T(8,128)(2,1)} %win_hbm.1, ...), custom_call_target="tpu_custom_call" | custom-call | tf_op jit(solution)/shard_map/ewald_step/pallas_call | solution.py:517
  40.0 0.6 %copy.15 = f32[8,128]{1,0:T(8,128)} copy(f32[8,128]{1,0:T(8,128)S(1)} %get-tuple-element.4) | data formatting | bytes 8192
  40.6 0.6 %copy.16 = f32[3,128]{1,0:T(4,128)} copy(f32[3,128]{1,0:T(4,128)S(1)} %get-tuple-element.5) | data formatting | bytes 3072
